TPU v7x, 128 devices: a whole 4x4x4 slice. The times are simulated.
128 devices in a mesh: seq: 16 (over y, x), chan: 8 (over z, core).
Axes of the slice: x: 4, y: 4, z: 4, core: 2. Of those that a mesh axis runs over, the one named last changes fastest.
Arguments:
- signal: bfloat16 [256, 32768], P('chan', 'seq'), may hold values from -6 to 6
- gate_values: bfloat16 [256, 32768], P('chan', 'seq'), may hold values from -6 to 6
- filter_taps: float32 [256, 32768], P('chan', 'seq'), may hold values from -6 to 6
- skip_gain: float32 [256], P('chan'), may hold values from 0.5 to 1.5
- positive: bfloat16 [256, 32768], P('chan', 'seq'), may hold values from -6 to 6
- item_table: bfloat16 [256, 524288], P('chan', 'seq'), may hold values from -6 to 6
- item_row: int32 [524288], replicated, may hold values from 0 to 524287, as said below
- negative_ids: int32 [256, 64], P('seq'), may hold values from 0 to 524287, as said below
- block_counts: int32 [256], P('seq'), may hold values from 1 to 64, 10240 in all
Outputs:
- grad_signal: float32 [256, 32768], P('chan', 'seq')
- grad_gate: bfloat16 [256, 32768], P('chan', 'seq')
- grad_filter: float32 [256, 32768], P('chan', 'seq')
- grad_table: float32 [256, 524288], P('chan', 'seq')
Inputs may be any that keep to these rules, and one draw needn't show every extreme that they name: `item_row`: A permutation of the item ids. `negative_ids`: of the 1024 ids in the blocks of one index of seq, at most 96 map under item_row to rows of one owner (row // 32768); one owner receives exactly 96 from every index of seq, and for every index some owner receives exactly 96. `block_counts`: the valid negatives of a block are the first ones of its row of negative_ids.
All inputs are finite; a program needn't handle non-finite values.
Results may differ from a plain program's by a relative error of at most 0.015.
Values may be sent and summed in bfloat16 or wider, within the bound.
A program may use at most 128 MiB of HBM per device.

v0:
```python
import jax
import jax.numpy as jnp
from jax import lax
from jax.sharding import PartitionSpec as P

C = 256
LCOLS = 128


def partner_2(value, axis, stride):
    mask = 2**stride
    pairs = [(source, source ^ mask) for source in range(lax.axis_size(axis))]
    return lax.ppermute(value, axis, pairs)


def rotor(indices, modulus):
    angle = 2.0 * jnp.pi / modulus * (indices % modulus).astype(jnp.float32)
    return (jnp.cos(angle), -jnp.sin(angle))


def grid_rotor(row_count, col_count, modulus):
    indices = (
        jnp.arange(row_count, dtype=jnp.int32)[:, None]
        * jnp.arange(col_count, dtype=jnp.int32)[None, :]
    )
    return rotor(indices, modulus)


def product(former, latter):
    return (
        former[0] * latter[0] - former[1] * latter[1],
        former[0] * latter[1] + former[1] * latter[0],
    )


def conjugate(complex_in):
    return (complex_in[0], -complex_in[1])


def contract(pattern, former, latter):

    def single(left_op, right_op):
        return jnp.einsum(
            pattern,
            left_op,
            right_op,
            precision=lax.Precision.HIGHEST,
            preferred_element_type=jnp.float32,
        )

    return (
        single(former[0], latter[0]) - single(former[1], latter[1]),
        single(former[0], latter[1]) + single(former[1], latter[0]),
    )


def local_forward(complex_in):
    row_count, length_all = complex_in[0].shape
    outer_len = length_all // LCOLS
    sectioned = (
        complex_in[0].reshape(row_count, outer_len, LCOLS),
        complex_in[1].reshape(row_count, outer_len, LCOLS),
    )
    sectioned = contract("kb,rbc->rkc", grid_rotor(outer_len, outer_len, outer_len), sectioned)
    sectioned = product(sectioned, grid_rotor(outer_len, LCOLS, length_all))
    sectioned = contract("rkc,cm->rkm", sectioned, grid_rotor(LCOLS, LCOLS, LCOLS))
    return (
        sectioned[0].reshape(row_count, length_all),
        sectioned[1].reshape(row_count, length_all),
    )


def local_inverse(complex_in):
    row_count, length_all = complex_in[0].shape
    outer_len = length_all // LCOLS
    sectioned = (
        complex_in[0].reshape(row_count, outer_len, LCOLS),
        complex_in[1].reshape(row_count, outer_len, LCOLS),
    )
    sectioned = contract("rkm,cm->rkc", sectioned, conjugate(grid_rotor(LCOLS, LCOLS, LCOLS)))
    sectioned = product(sectioned, conjugate(grid_rotor(outer_len, LCOLS, length_all)))
    sectioned = contract(
        "kb,rkc->rbc", conjugate(grid_rotor(outer_len, outer_len, outer_len)), sectioned
    )
    inverse_len = 1.0 / length_all
    return (
        sectioned[0].reshape(row_count, length_all) * inverse_len,
        sectioned[1].reshape(row_count, length_all) * inverse_len,
    )


def reversed_bits(device_at, levels):
    result = jnp.zeros((), jnp.int32)
    for level_bit in range(levels):
        result = result + (device_at >> level_bit & 1) * (1 << levels - 1 - level_bit)
    return result


def frequency_held(piece_count, device_at):
    return reversed_bits(device_at, piece_count.bit_length() - 1)


def cross_forward(complex_in, piece_count, device_at):
    stacked = jnp.stack(complex_in)
    levels = piece_count.bit_length() - 1
    for level_bit in range(levels - 1, -1, -1):
        half_span = 1 << level_bit
        partner = partner_2(stacked, "seq", level_bit)
        is_upper = device_at >> level_bit & 1 == 1
        phase_turn = rotor(device_at & half_span - 1, 2 * half_span)
        differ = partner - stacked
        rotated = jnp.stack(product((differ[0], differ[1]), phase_turn))
        stacked = jnp.where(is_upper, rotated, stacked + partner)
    return (stacked[0], stacked[1])


def cross_inverse(complex_in, piece_count, device_at):
    stacked = jnp.stack(complex_in)
    levels = piece_count.bit_length() - 1
    for level_bit in range(levels):
        half_span = 1 << level_bit
        is_upper = device_at >> level_bit & 1 == 1
        phase_turn = conjugate(rotor(device_at & half_span - 1, 2 * half_span))
        twisted = jnp.where(
            is_upper, jnp.stack(product((stacked[0], stacked[1]), phase_turn)), stacked
        )
        partner = partner_2(twisted.astype(jnp.bfloat16), "seq", level_bit).astype(twisted.dtype)
        stacked = 0.5 * jnp.where(is_upper, partner - twisted, twisted + partner)
    return (stacked[0], stacked[1])


def spectrum_of(complex_in, piece_count, device_at):
    complex_in = cross_forward(complex_in, piece_count, device_at)
    width_here = complex_in[0].shape[1]
    held_freq = frequency_held(piece_count, device_at)
    indices = jnp.arange(width_here, dtype=jnp.int32) * held_freq
    complex_in = product(complex_in, rotor(indices, piece_count * width_here))
    return local_forward(complex_in)


def positions_of(complex_in, piece_count, device_at):
    complex_in = local_inverse(complex_in)
    width_here = complex_in[0].shape[1]
    held_freq = frequency_held(piece_count, device_at)
    indices = jnp.arange(width_here, dtype=jnp.int32) * held_freq
    complex_in = product(complex_in, conjugate(rotor(indices, piece_count * width_here)))
    complex_in = cross_inverse(complex_in, piece_count, device_at)
    return complex_in


def local(
    signal,
    gate_values,
    filter_taps,
    skip_gain,
    positive,
    item_table,
    item_row,
    negative_ids,
    block_counts,
):
    channels, length = signal.shape
    seq_parts = lax.axis_size("seq")
    filter_scale = (seq_parts * length) ** (-0.5)
    score_scale = C ** (-0.5)
    source = signal.astype(jnp.float32)
    gating = gate_values.astype(jnp.float32)
    source_here, taps_here = (source, filter_taps)
    device_at = lax.axis_index("seq")
    rows_here, width_here = source_here.shape
    phase_n = rotor(
        device_at * width_here + jnp.arange(width_here, dtype=jnp.int32), 2 * seq_parts * width_here
    )

    def split_rows(items_list):
        real_rows = []
        imag_rows = []
        for values in items_list:
            real_rows += [values, values * phase_n[0]]
            imag_rows += [jnp.zeros_like(values), values * phase_n[1]]
        return (jnp.concatenate(real_rows), jnp.concatenate(imag_rows))

    def combine(complex_in, item_total):
        results = []
        for item_no in range(item_total):
            even_part = complex_in[0][2 * item_no * rows_here : (2 * item_no + 1) * rows_here]
            odd_real = complex_in[0][(2 * item_no + 1) * rows_here : (2 * item_no + 2) * rows_here]
            odd_imag = complex_in[1][(2 * item_no + 1) * rows_here : (2 * item_no + 2) * rows_here]
            results.append(0.5 * (even_part + phase_n[0] * odd_real + phase_n[1] * odd_imag))
        return results

    spectra = spectrum_of(split_rows([source_here, taps_here]), seq_parts, device_at)
    signal_spec = (spectra[0][: 2 * rows_here], spectra[1][: 2 * rows_here])
    taps_spec = (spectra[0][2 * rows_here :], spectra[1][2 * rows_here :])
    conv_here = (
        filter_scale
        * combine(positions_of(product(signal_spec, taps_spec), seq_parts, device_at), 1)[0]
    )
    pre_gate = conv_here + skip_gain[:, None] * source
    encoded = (gating * pre_gate).astype(jnp.bfloat16)
    blocks, neg_width = negative_ids.shape
    block_len = length // blocks
    slots = blocks * neg_width
    capacity = (3 * slots + 2 * seq_parts - 1) // (2 * seq_parts)
    rows_own = item_table.shape[1]
    neg_rows = item_row[negative_ids].reshape(slots)
    owner_of = neg_rows // rows_own
    local_row = neg_rows % rows_own
    onehot = (owner_of[:, None] == jnp.arange(seq_parts, dtype=jnp.int32)[None, :]).astype(
        jnp.int32
    )
    slot_rank = jnp.sum((jnp.cumsum(onehot, axis=0) - onehot) * onehot, axis=1)
    requests = jnp.zeros((seq_parts, capacity), jnp.int32).at[owner_of, slot_rank].set(local_row)
    asked_rows = lax.all_to_all(requests, "seq", split_axis=0, concat_axis=0, tiled=True)
    found_rows = jnp.transpose(jnp.take(item_table, asked_rows, axis=1), (1, 2, 0))
    returned = lax.all_to_all(found_rows, "seq", split_axis=0, concat_axis=0, tiled=True)
    asked_rows, fetched = (asked_rows, returned)
    neg_embed = fetched[owner_of, slot_rank].reshape(blocks, neg_width, channels)
    enc_blocks = encoded.reshape(channels, blocks, block_len)
    part_neg = jnp.einsum("bjc,cbt->btj", neg_embed, enc_blocks, preferred_element_type=jnp.float32)
    part_pos = jnp.einsum("ct,ct->t", encoded, positive, preferred_element_type=jnp.float32)
    score_neg, score_pos = (
        lax.psum(part_neg.astype(jnp.bfloat16), "chan").astype(jnp.float32),
        lax.psum(part_pos.astype(jnp.bfloat16), "chan").astype(jnp.float32),
    )
    score_neg = score_scale * score_neg
    score_pos = score_scale * score_pos
    is_valid = jnp.arange(neg_width, dtype=jnp.int32)[None, None, :] < block_counts[:, None, None]
    neg_weight = jnp.where(is_valid, jax.nn.sigmoid(score_neg), 0.0).astype(jnp.bfloat16)
    pos_weight = -jax.nn.sigmoid(-score_pos)
    from_negs = jnp.einsum(
        "btj,bjc->cbt", neg_weight, neg_embed, preferred_element_type=jnp.float32
    )
    enc_grad = score_scale * (
        pos_weight[None, :] * positive.astype(jnp.float32) + from_negs.reshape(channels, length)
    )
    slot_grad = score_scale * jnp.einsum(
        "btj,cbt->bjc", neg_weight, enc_blocks, preferred_element_type=jnp.float32
    ).reshape(slots, channels)
    outgoing = (
        jnp.zeros((seq_parts, capacity, channels), jnp.float32)
        .at[owner_of, slot_rank]
        .set(slot_grad)
    )
    incoming = lax.all_to_all(
        outgoing.astype(jnp.bfloat16), "seq", split_axis=0, concat_axis=0, tiled=True
    ).astype(outgoing.dtype)
    grad_table = (
        jnp.zeros((channels, rows_own), jnp.float32)
        .at[:, asked_rows.reshape(-1)]
        .add(jnp.transpose(incoming.reshape(-1, channels)))
    )
    grad_gate = (enc_grad * pre_gate).astype(jnp.bfloat16)
    gate_back = enc_grad * gating
    back_spec = spectrum_of(split_rows([gate_back]), seq_parts, device_at)
    with_taps = product(conjugate(taps_spec), back_spec)
    with_signal = product(conjugate(signal_spec), back_spec)
    joined = (
        jnp.concatenate([with_taps[0], with_signal[0]]),
        jnp.concatenate([with_taps[1], with_signal[1]]),
    )
    lag_results = combine(positions_of(joined, seq_parts, device_at), 2)
    lag_taps = filter_scale * lag_results[0]
    lag_signal = filter_scale * lag_results[1]
    grad_signal = lag_taps + skip_gain[:, None] * gate_back
    return (grad_signal, grad_gate, lag_signal, grad_table)


def solution(mesh):
    in_specs = (
        P("chan", "seq"),
        P("chan", "seq"),
        P("chan", "seq"),
        P("chan"),
        P("chan", "seq"),
        P("chan", "seq"),
        P(),
        P("seq", None),
        P("seq"),
    )
    out_specs = (P("chan", "seq"), P("chan", "seq"), P("chan", "seq"), P("chan", "seq"))
    return jax.shard_map(local, mesh=mesh, in_specs=in_specs, out_specs=out_specs, check_vma=False)
```

profile of v0, /device:TPU:96, one launch (start us, length us, event | category | flops | bytes accessed | tf_op | source)
XLA Modules:
  0.0 667.0 jit_solution(16556857119814001588)
XLA Ops:
  15.7 45.8 %collective-permute-done = f32[2,128,2048]{2,1,0:T(8,128)} collective-permute-done((f32[2,128,2048]{2,1,0:T(8,128)}, f32[2,128,2048]{2,1,0:T(8,128)}, u32[]{:S(2)}, u32[]{:S(2)}) %collective-permute-start) | collective-permute-done | bytes 2097184 | tf_op jit(solution)/shard_map/ppermute | solution.py:13
  64.8 3.5 maximum_select_fusion
  70.0 45.1 %collective-permute-done.1 = f32[2,128,2048]{2,1,0:T(8,128)} collective-permute-done((f32[2,128,2048]{2,1,0:T(8,128)}, f32[2,128,2048]{2,1,0:T(8,128)}, u32[]{:S(2)}, u32[]{:S(2)}) %collective-permute-start.1) | collective-permute-done | bytes 2097184 | tf_op jit(solution)/shard_map/ppermute | solution.py:13
  115.1 3.9 fusion.365
  120.9 4.6 maximum_select_fusion.1
  128.7 44.2 %collective-permute-done.2 = f32[2,128,2048]{2,1,0:T(8,128)} collective-permute-done((f32[2,128,2048]{2,1,0:T(8,128)}, f32[2,128,2048]{2,1,0:T(8,128)}, u32[]{:S(2)}, u32[]{:S(2)}) %collective-permute-start.2) | collective-permute-done | bytes 2097184 | tf_op jit(solution)/shard_map/ppermute | solution.py:13
  175.7 4.1 maximum_select_fusion.2
  181.4 6.6 gather_fusion
  188.3 36.4 %collective-permute-done.3 = f32[2,128,2048]{2,1,0:T(8,128)} collective-permute-done((f32[2,128,2048]{2,1,0:T(8,128)}, f32[2,128,2048]{2,1,0:T(8,128)}, u32[]{:S(2)}, u32[]{:S(2)}) %collective-permute-start.3) | collective-permute-done | bytes 2097184 | tf_op jit(solution)/shard_map/ppermute | solution.py:13
  251.7 4.5 reduce-window.6
  256.6 3.8 collective-permute-done.4
  265.3 8.6 %collective-permute-done.5 = bf16[2,64,2048]{2,1,0:T(8,128)(2,1)S(1)} collective-permute-done((bf16[2,64,2048]{2,1,0:T(8,128)(2,1)S(1)}, bf16[2,64,2048]{2,1,0:T(8,128)(2,1)S(1)}, u32[]{:S(2)}, u32[]{:S(2)}) %collective-permute-start.5) | collective-permute-done | bytes 524320 | tf_op jit(solution)/shard_map/ppermute | solution.py:13
  277.5 4.3 scatter_custom_fusion.1
  282.5 6.7 %all-to-all-start = ((s32[16,1,96]{2,1,0:T(1,128)}), s32[16,1,96]{2,1,0:T(1,128)S(1)}, u32[]{:S(2)}, u32[]{:S(2)}) async-start(s32[16,1,96]{2,1,0:T(1,128)} %all_to_all.16), calls=%async_computation | async-start | bytes 16384 | tf_op jit(solution)/shard_map/all_to_all | solution.py:214
  289.2 7.4 %copy.166 = bf16[32,32768]{0,1:T(8,128)(2,1)} copy(bf16[32,32768]{1,0:T(8,128)(2,1)} %param.14) | data formatting | bytes 4194304 | tf_op args[5]
  302.7 7.1 %gather_fusion.1 = bf16[1536,32]{1,0:T(8,128)(2,1)S(1)} fusion(bf16[32,32768]{0,1:T(8,128)(2,1)} %copy.166, s32[2048]{0:T(1024)S(1)} %pad_clamp_fusion), kind=kCustom, calls=%fused_computation.1 | custom fusion | bytes 202752 | tf_op jit(solution)/shard_map/jit(_take)/gather | solution.py:215
  310.7 4.9 all-to-all-start.1
  315.8 7.9 %all-to-all-done.1 = bf16[16,96,32]{1,2,0:T(8,128)(2,1)S(1)} async-done(((bf16[16,96,32]{1,2,0:T(8,128)(2,1)}), bf16[16,96,32]{1,2,0:T(8,128)(2,1)S(1)}, u32[]{:S(2)}, u32[]{:S(2)}) %all-to-all-start.1) | async-done | bytes 98336 | tf_op jit(solution)/shard_map/all_to_all | solution.py:216
  323.8 5.8 gather_fusion.2
  330.9 10.1 %psum.14 = bf16[2048]{0:T(1024)(128)(2,1)S(1)} all-reduce(bf16[2048]{0:T(1024)(128)(2,1)S(1)} %get-tuple-element.29), channel_id=1, replica_groups=mesh['seq'=16,'chan'=8] {'chan'}, use_global_device_ids=true, to_apply=%region_0.1 | all-reduce | flops 2048 | bytes 8192 | tf_op jit(solution)/shard_map/psum | solution.py:224
  342.0 55.2 %all-reduce.3.cloned.1.call-done = bf16[16,128,64]{1,2,0:T(8,128)(2,1)} async-done(((bf16[16,128,64]{1,2,0:T(8,128)(2,1)}), bf16[16,128,64]{1,2,0:T(8,128)(2,1)}) %all-reduce.3.cloned.1.call-update) | async-done | bytes 262160 | tf_op jit(solution)/shard_map/psum | solution.py:223
  402.6 24.3 %collective-permute-done.8 = f32[2,64,2048]{2,1,0:T(8,128)S(1)} collective-permute-done((f32[2,64,2048]{2,1,0:T(8,128)S(1)}, f32[2,64,2048]{2,1,0:T(8,128)S(1)}, u32[]{:S(2)}, u32[]{:S(2)}) %collective-permute-start.8) | collective-permute-done | bytes 1048608 | tf_op jit(solution)/shard_map/ppermute | solution.py:13
  428.9 23.4 %collective-permute-done.9 = f32[2,64,2048]{2,1,0:T(8,128)S(1)} collective-permute-done((f32[2,64,2048]{2,1,0:T(8,128)S(1)}, f32[2,64,2048]{2,1,0:T(8,128)S(1)}, u32[]{:S(2)}, u32[]{:S(2)}) %collective-permute-start.9) | collective-permute-done | bytes 1048608 | tf_op jit(solution)/shard_map/ppermute | solution.py:13
  456.3 22.6 %collective-permute-done.10 = f32[2,64,2048]{2,1,0:T(8,128)S(1)} collective-permute-done((f32[2,64,2048]{2,1,0:T(8,128)S(1)}, f32[2,64,2048]{2,1,0:T(8,128)S(1)}, u32[]{:S(2)}, u32[]{:S(2)}) %collective-permute-start.10) | collective-permute-done | bytes 1048608 | tf_op jit(solution)/shard_map/ppermute | solution.py:13
  481.4 21.7 %collective-permute-done.11 = f32[2,64,2048]{2,1,0:T(8,128)S(1)} collective-permute-done((f32[2,64,2048]{2,1,0:T(8,128)S(1)}, f32[2,64,2048]{2,1,0:T(8,128)S(1)}, u32[]{:S(2)}, u32[]{:S(2)}) %collective-permute-start.11) | collective-permute-done | bytes 1048608 | tf_op jit(solution)/shard_map/ppermute | solution.py:13
  534.5 20.8 %collective-permute-done.12 = bf16[2,128,2048]{2,1,0:T(8,128)(2,1)S(1)} collective-permute-done((bf16[2,128,2048]{2,1,0:T(8,128)(2,1)S(1)}, bf16[2,128,2048]{2,1,0:T(8,128)(2,1)S(1)}, u32[]{:S(2)}, u32[]{:S(2)}) %collective-permute-start.12) | collective-permute-done | bytes 1048608 | tf_op jit(solution)/shard_map/ppermute | solution.py:13
  560.1 19.8 %collective-permute-done.13 = bf16[2,128,2048]{2,1,0:T(8,128)(2,1)S(1)} collective-permute-done((bf16[2,128,2048]{2,1,0:T(8,128)(2,1)S(1)}, bf16[2,128,2048]{2,1,0:T(8,128)(2,1)S(1)}, u32[]{:S(2)}, u32[]{:S(2)}) %collective-permute-start.13) | collective-permute-done | bytes 1048608 | tf_op jit(solution)/shard_map/ppermute | solution.py:13
  583.3 18.9 %collective-permute-done.14 = bf16[2,128,2048]{2,1,0:T(8,128)(2,1)S(1)} collective-permute-done((bf16[2,128,2048]{2,1,0:T(8,128)(2,1)S(1)}, bf16[2,128,2048]{2,1,0:T(8,128)(2,1)S(1)}, u32[]{:S(2)}, u32[]{:S(2)}) %collective-permute-start.14) | collective-permute-done | bytes 1048608 | tf_op jit(solution)/shard_map/ppermute | solution.py:13
  615.5 4.8 all-to-all-start.2
  620.3 8.0 %all-to-all-done.2 = bf16[16,96,32]{1,2,0:T(8,128)(2,1)S(1)} async-done(((bf16[16,96,32]{1,2,0:T(8,128)(2,1)}), bf16[16,96,32]{1,2,0:T(8,128)(2,1)S(1)}, u32[]{:S(2)}, u32[]{:S(2)}) %all-to-all-start.2) | async-done | bytes 98336 | tf_op jit(solution)/shard_map/all_to_all | solution.py:245
  628.4 16.1 %scatter_custom_fusion = f32[32,32768]{0,1:T(8,128)} fusion(s32[1536]{0:T(1024)S(1)} %fusion.191, f32[1536,32]{1,0:T(8,128)S(1)} %bitcast.303, f32[]{:T(128)} %constant.246.clone.1), kind=kCustom, calls=%fused_computation.6 | custom fusion | flops 49152 | bytes 4194308 | tf_op jit(solution)/shard_map/scatter-add | solution.py:251
  644.5 11.6 %copy.191 = f32[32,32768]{1,0:T(8,128)} copy(f32[32,32768]{0,1:T(8,128)} %scatter_custom_fusion) | data formatting | bytes 8388608
  (270 shorter events, 138.5 us)
Async XLA Ops:
  7.2 174.2 %copy-start = (s32[524288]{0:T(1024)S(1)}, s32[524288]{0:T(1024)}, u32[]{:S(2)}) copy-start(s32[524288]{0:T(1024)} %param.15) | copy-start | bytes 6291460
  12.3 49.2 %collective-permute-start = (f32[2,128,2048]{2,1,0:T(8,128)}, f32[2,128,2048]{2,1,0:T(8,128)}, u32[]{:S(2)}, u32[]{:S(2)}) collective-permute-start(f32[2,128,2048]{2,1,0:T(8,128)} %pad_maximum_fusion), channel_id=1, source_target_pairs={{0,64},{8,72},{16,80},{24,88},{32,96},{40,104},{48,112},{56,120},{... | collective-permute-start | bytes 6291464 | tf_op jit(solution)/shard_map/ppermute | solution.py:13
  68.3 46.8 %collective-permute-start.1 = (f32[2,128,2048]{2,1,0:T(8,128)}, f32[2,128,2048]{2,1,0:T(8,128)}, u32[]{:S(2)}, u32[]{:S(2)}) collective-permute-start(f32[2,128,2048]{2,1,0:T(8,128)} %maximum_select_fusion), channel_id=1, source_target_pairs={{0,32},{8,40},{16,48},{24,56},{32,0},{40,8},{48,16},{56,24},{64,96... | collective-permute-start | bytes 6291464 | tf_op jit(solution)/shard_map/ppermute | solution.py:13
  125.5 47.4 %collective-permute-start.2 = (f32[2,128,2048]{2,1,0:T(8,128)}, f32[2,128,2048]{2,1,0:T(8,128)}, u32[]{:S(2)}, u32[]{:S(2)}) collective-permute-start(f32[2,128,2048]{2,1,0:T(8,128)} %maximum_select_fusion.1), channel_id=1, source_target_pairs={{0,16},{8,24},{16,0},{24,8},{32,48},{40,56},{48,32},{56,40},{64,80... | collective-permute-start | bytes 6291464 | tf_op jit(solution)/shard_map/ppermute | solution.py:13
  179.8 45.0 %collective-permute-start.3 = (f32[2,128,2048]{2,1,0:T(8,128)}, f32[2,128,2048]{2,1,0:T(8,128)}, u32[]{:S(2)}, u32[]{:S(2)}) collective-permute-start(f32[2,128,2048]{2,1,0:T(8,128)} %maximum_select_fusion.2), channel_id=1, source_target_pairs={{0,8},{8,0},{16,24},{24,16},{32,40},{40,32},{48,56},{56,48},{64,72... | collective-permute-start | bytes 6291464 | tf_op jit(solution)/shard_map/ppermute | solution.py:13
  188.1 60.7 %copy-start.30 = (f32[2048]{0:T(1024)}, f32[2048]{0:T(1024)S(1)}, u32[]{:S(2)}) copy-start(f32[2048]{0:T(1024)S(1)} %get-tuple-element.96) | copy-start | bytes 24580
  188.1 60.7 %copy-start.32 = (f32[2048]{0:T(1024)}, f32[2048]{0:T(1024)S(1)}, u32[]{:S(2)}) copy-start(f32[2048]{0:T(1024)S(1)} %get-tuple-element.97) | copy-start | bytes 24580
  188.2 42.6 %copy-start.36 = (f32[16,128]{1,0:T(8,128)}, f32[16,128]{1,0:T(8,128)S(1)}, u32[]{:S(2)}) copy-start(f32[16,128]{1,0:T(8,128)S(1)} %get-tuple-element.98) | copy-start | bytes 24580
  188.2 42.6 %copy-start.38 = (f32[16,128]{1,0:T(8,128)}, f32[16,128]{1,0:T(8,128)S(1)}, u32[]{:S(2)}) copy-start(f32[16,128]{1,0:T(8,128)S(1)} %get-tuple-element.99) | copy-start | bytes 24580
  188.3 46.0 %copy-start.34 = (f32[16,128]{1,0:T(8,128)}, f32[16,128]{1,0:T(8,128)S(1)}, u32[]{:S(2)}) copy-start(f32[16,128]{1,0:T(8,128)S(1)} %get-tuple-element.101) | copy-start | bytes 24580
  249.1 11.7 %copy-start.10 = (f32[1,64,2048]{2,1,0:T(8,128)}, f32[1,64,2048]{2,1,0:T(8,128)S(1)}, u32[]{:S(2)}) copy-start(f32[1,64,2048]{2,1,0:T(8,128)S(1)} %multiply_add_fusion.21) | copy-start | bytes 1572868
  250.2 10.2 %collective-permute-start.4 = (bf16[2,64,2048]{2,1,0:T(8,128)(2,1)}, bf16[2,64,2048]{2,1,0:T(8,128)(2,1)S(1)}, u32[]{:S(2)}, u32[]{:S(2)}) collective-permute-start(bf16[2,64,2048]{2,1,0:T(8,128)(2,1)} %fusion.91), channel_id=1, source_target_pairs={{0,8},{8,0},{16,24},{24,16},{32,40},{40,32},{48,56},{56,48},{64,72... | collective-permute-start | bytes 1572872 | tf_op jit(solution)/shard_map/ppermute | solution.py:13
  261.6 12.3 %collective-permute-start.5 = (bf16[2,64,2048]{2,1,0:T(8,128)(2,1)S(1)}, bf16[2,64,2048]{2,1,0:T(8,128)(2,1)S(1)}, u32[]{:S(2)}, u32[]{:S(2)}) collective-permute-start(bf16[2,64,2048]{2,1,0:T(8,128)(2,1)S(1)} %fusion.63), channel_id=1, source_target_pairs={{0,16},{8,24},{16,0},{24,8},{32,48},{40,56},{48,32},{56,40},{64,80... | collective-permute-start | bytes 1572872 | tf_op jit(solution)/shard_map/ppermute | solution.py:13
  275.6 21.0 %copy-start.17 = (f32[1,64,2048]{2,1,0:T(8,128)}, f32[1,64,2048]{2,1,0:T(8,128)S(1)}, u32[]{:S(2)}) copy-start(f32[1,64,2048]{2,1,0:T(8,128)S(1)} %get-tuple-element.81) | copy-start | bytes 1572868
  275.8 21.0 %collective-permute-start.6 = (bf16[2,64,2048]{2,1,0:T(8,128)(2,1)S(1)}, bf16[2,64,2048]{2,1,0:T(8,128)(2,1)}, u32[]{:S(2)}, u32[]{:S(2)}) collective-permute-start(bf16[2,64,2048]{2,1,0:T(8,128)(2,1)S(1)} %fusion.62), channel_id=1, source_target_pairs={{0,32},{8,40},{16,48},{24,56},{32,0},{40,8},{48,16},{56,24},{64,96... | collective-permute-start | bytes 1572872 | tf_op jit(solution)/shard_map/ppermute | solution.py:13
  277.5 19.1 %copy-start.41 = (s32[1024]{0:T(1024)}, s32[1024]{0:T(1024)S(1)}, u32[]{:S(2)}) copy-start(s32[1024]{0:T(1024)S(1)} %broadcast_select_fusion.1) | copy-start | bytes 12292
  282.5 14.2 %all-to-all-start = ((s32[16,1,96]{2,1,0:T(1,128)}), s32[16,1,96]{2,1,0:T(1,128)S(1)}, u32[]{:S(2)}, u32[]{:S(2)}) async-start(s32[16,1,96]{2,1,0:T(1,128)} %all_to_all.16), calls=%async_computation | async-start | bytes 16384 | tf_op jit(solution)/shard_map/all_to_all | solution.py:214
  298.3 17.3 %copy-start.46 = (s32[16]{0:T(128)S(1)}, s32[16]{0:T(128)}, u32[]{:S(2)}) copy-start(s32[16]{0:T(128)} %param.17) | copy-start | bytes 196
  299.3 30.5 %collective-permute-start.7 = (bf16[2,64,2048]{2,1,0:T(8,128)(2,1)}, bf16[2,64,2048]{2,1,0:T(8,128)(2,1)S(1)}, u32[]{:S(2)}, u32[]{:S(2)}) collective-permute-start(bf16[2,64,2048]{2,1,0:T(8,128)(2,1)} %fusion.61), channel_id=1, source_target_pairs={{0,64},{8,72},{16,80},{24,88},{32,96},{40,104},{48,112},{56,120},{... | collective-permute-start | bytes 1572872 | tf_op jit(solution)/shard_map/ppermute | solution.py:13
  310.7 12.9 %all-to-all-start.1 = ((bf16[16,96,32]{1,2,0:T(8,128)(2,1)}), bf16[16,96,32]{1,2,0:T(8,128)(2,1)S(1)}, u32[]{:S(2)}, u32[]{:S(2)}) async-start(bf16[16,96,32]{1,2,0:T(8,128)(2,1)} %broadcast_select_fusion), calls=%async_computation.1 | async-start | bytes 262144 | tf_op jit(solution)/shard_map/all_to_all | solution.py:216
  315.6 81.6 %all-reduce.3.cloned.1.call-start = ((), (), s32[]{:S(2)}) async-start(), calls=%async_computation.3 | async-start | bytes 524288 | tf_op jit(solution)/shard_map/psum | solution.py:223
  315.8 81.5 %copy-start.42 = (pred[16,64]{1,0:T(8,128)(4,1)}, pred[16,64]{1,0:T(8,128)(4,1)S(1)}, u32[]{:S(2)}) copy-start(pred[16,64]{1,0:T(8,128)(4,1)S(1)} %iota_compare_fusion.2) | copy-start | bytes 3076
  330.9 68.4 %copy-start.18 = (f32[32,2048]{1,0:T(8,128)}, f32[32,2048]{1,0:T(8,128)S(1)}, u32[]{:S(2)}) copy-start(f32[32,2048]{1,0:T(8,128)S(1)} %get-tuple-element.30) | copy-start | bytes 786436
  399.5 27.4 %collective-permute-start.8 = (f32[2,64,2048]{2,1,0:T(8,128)S(1)}, f32[2,64,2048]{2,1,0:T(8,128)S(1)}, u32[]{:S(2)}, u32[]{:S(2)}) collective-permute-start(f32[2,64,2048]{2,1,0:T(8,128)S(1)} %pad_maximum_fusion.1), channel_id=1, source_target_pairs={{0,64},{8,72},{16,80},{24,88},{32,96},{40,104},{48,112},{56,120},{... | collective-permute-start | bytes 3145736 | tf_op jit(solution)/shard_map/ppermute | solution.py:13
  427.4 25.0 %collective-permute-start.9 = (f32[2,64,2048]{2,1,0:T(8,128)S(1)}, f32[2,64,2048]{2,1,0:T(8,128)S(1)}, u32[]{:S(2)}, u32[]{:S(2)}) collective-permute-start(f32[2,64,2048]{2,1,0:T(8,128)S(1)} %maximum_select_fusion.12), channel_id=1, source_target_pairs={{0,32},{8,40},{16,48},{24,56},{32,0},{40,8},{48,16},{56,24},{64,96... | collective-permute-start | bytes 3145736 | tf_op jit(solution)/shard_map/ppermute | solution.py:13
  453.2 25.6 %collective-permute-start.10 = (f32[2,64,2048]{2,1,0:T(8,128)S(1)}, f32[2,64,2048]{2,1,0:T(8,128)S(1)}, u32[]{:S(2)}, u32[]{:S(2)}) collective-permute-start(f32[2,64,2048]{2,1,0:T(8,128)S(1)} %maximum_select_fusion.13), channel_id=1, source_target_pairs={{0,16},{8,24},{16,0},{24,8},{32,48},{40,56},{48,32},{56,40},{64,80... | collective-permute-start | bytes 3145736 | tf_op jit(solution)/shard_map/ppermute | solution.py:13
  479.4 23.6 %collective-permute-start.11 = (f32[2,64,2048]{2,1,0:T(8,128)S(1)}, f32[2,64,2048]{2,1,0:T(8,128)S(1)}, u32[]{:S(2)}, u32[]{:S(2)}) collective-permute-start(f32[2,64,2048]{2,1,0:T(8,128)S(1)} %maximum_select_fusion.14), channel_id=1, source_target_pairs={{0,8},{8,0},{16,24},{24,16},{32,40},{40,32},{48,56},{56,48},{64,72... | collective-permute-start | bytes 3145736 | tf_op jit(solution)/shard_map/ppermute | solution.py:13
  533.0 22.3 %collective-permute-start.12 = (bf16[2,128,2048]{2,1,0:T(8,128)(2,1)S(1)}, bf16[2,128,2048]{2,1,0:T(8,128)(2,1)S(1)}, u32[]{:S(2)}, u32[]{:S(2)}) collective-permute-start(bf16[2,128,2048]{2,1,0:T(8,128)(2,1)S(1)} %fusion.84), channel_id=1, source_target_pairs={{0,8},{8,0},{16,24},{24,16},{32,40},{40,32},{48,56},{56,48},{64,72... | collective-permute-start | bytes 3145736 | tf_op jit(solution)/shard_map/ppermute | solution.py:13
  557.0 22.9 %collective-permute-start.13 = (bf16[2,128,2048]{2,1,0:T(8,128)(2,1)S(1)}, bf16[2,128,2048]{2,1,0:T(8,128)(2,1)S(1)}, u32[]{:S(2)}, u32[]{:S(2)}) collective-permute-start(bf16[2,128,2048]{2,1,0:T(8,128)(2,1)S(1)} %fusion.42), channel_id=1, source_target_pairs={{0,16},{8,24},{16,0},{24,8},{32,48},{40,56},{48,32},{56,40},{64,80... | collective-permute-start | bytes 3145736 | tf_op jit(solution)/shard_map/ppermute | solution.py:13
  581.5 20.7 %collective-permute-start.14 = (bf16[2,128,2048]{2,1,0:T(8,128)(2,1)S(1)}, bf16[2,128,2048]{2,1,0:T(8,128)(2,1)S(1)}, u32[]{:S(2)}, u32[]{:S(2)}) collective-permute-start(bf16[2,128,2048]{2,1,0:T(8,128)(2,1)S(1)} %fusion.41), channel_id=1, source_target_pairs={{0,32},{8,40},{16,48},{24,56},{32,0},{40,8},{48,16},{56,24},{64,96... | collective-permute-start | bytes 3145736 | tf_op jit(solution)/shard_map/ppermute | solution.py:13
  605.3 50.8 %collective-permute-start.15 = (bf16[2,128,2048]{2,1,0:T(8,128)(2,1)}, bf16[2,128,2048]{2,1,0:T(8,128)(2,1)}, u32[]{:S(2)}, u32[]{:S(2)}) collective-permute-start(bf16[2,128,2048]{2,1,0:T(8,128)(2,1)} %fusion.40), channel_id=1, source_target_pairs={{0,64},{8,72},{16,80},{24,88},{32,96},{40,104},{48,112},{56,120},{... | collective-permute-start | bytes 3145736 | tf_op jit(solution)/shard_map/ppermute | solution.py:13
  615.5 12.8 %all-to-all-start.2 = ((bf16[16,96,32]{1,2,0:T(8,128)(2,1)}), bf16[16,96,32]{1,2,0:T(8,128)(2,1)S(1)}, u32[]{:S(2)}, u32[]{:S(2)}) async-start(bf16[16,96,32]{1,2,0:T(8,128)(2,1)} %copy.188), calls=%async_computation.2 | async-start | bytes 262144 | tf_op jit(solution)/shard_map/all_to_all | solution.py:245
  (37 other events, 85.9 us)
Sparse Core Ops, SparseCore 0:
  342.1 55.0 all-reduce.2
where the time goes:
time: 673 us; the launch traced here: 667 us
  waiting for transfers between devices  406 us (60%)
  other arithmetic  76.5 us (11%)
  local copies, waits for them, and re-layouts  59.7 us (9%)
  starting transfers between devices  54.8 us (8%)
  matrix products  43.4 us (6%)
  between operations  16.1 us (2%)
  blocking collectives  10.1 us (2%)
    ppermute x16, waiting for transfers between devices, partner_2(): return lax.ppermute(value, axis, pairs)  335 us
    psum x1, waiting for transfers between devices, local(): lax.psum(part_neg.astype(jnp.bfloat16), 'chan').astype(jnp.float32)  55.2 us
    dot_general x32, matrix products, single(): jnp.einsum(pattern, left_op, right_op, precision=lax.Precision.HIGHEST, p...  39.7 us
    ppermute x16, starting transfers between devices, partner_2(): return lax.ppermute(value, axis, pairs)  38.4 us
    unnamed x108, local copies, waits for them, and re-layouts  32.8 us
    scatter-add x1, other arithmetic, local(): grad_table = jnp.zeros((channels, rows_own), jnp.float32).at[:, asked_row...  16.1 us
    select_n x8, other arithmetic, cross_forward(): stacked = jnp.where(is_upper, rotated, stacked + partner)  16 us
  transfers between devices with their start and end apart: 20, of which 16 were waited for; matrix products, arithmetic and copies ran while one was open for 11% of the time, Pallas kernels for 0%

commit v1 on v0

v1 whole, which is shorter than its diff:
```python
import functools

import jax
import jax.numpy as jnp
import ml_dtypes
import numpy as np
from jax import lax
from jax.experimental import pallas as pl
from jax.experimental.pallas import tpu as pltpu
from jax.sharding import PartitionSpec as P

C = 256
F32, BF16, I32 = jnp.float32, jnp.bfloat16, jnp.int32
VMEM = pl.BlockSpec(memory_space=pltpu.VMEM)
SMEM = pl.BlockSpec(memory_space=pltpu.SMEM)
N1, N2 = 256, 128
LIMIT = 56 * 1024 * 1024
NT = (((1,), (1,)), ((), ()))
TN = (((0,), (0,)), ((), ()))


def halves(matrix):
    high = matrix.astype(ml_dtypes.bfloat16)
    return high, (matrix - high.astype(np.float64)).astype(ml_dtypes.bfloat16)


def transform_tables():
    total = N1 * N2
    k1, n1 = np.arange(N1) + 0.25, np.arange(N1)
    n2 = np.arange(N2)
    first = np.exp(-2j * np.pi * np.outer(k1, n1) / N1)
    turn = np.exp(-2j * np.pi * np.outer(k1, n2) / total)
    last = np.exp(-2j * np.pi * np.outer(n2, n2) / N2)
    fwd1 = np.concatenate(halves(np.concatenate([first.real, first.imag])), axis=1)
    fwd2 = np.block([[last.real, last.imag], [-last.imag, last.real]])
    inv2 = np.block([[last.real, -last.imag], [last.imag, last.real]])
    inv1 = np.concatenate([first.real.T, first.imag.T], axis=1) / total

    def stack_k(matrix):
        high, low = halves(matrix)
        return np.concatenate([high, high, low])

    high, low = halves(inv1)
    inv1 = np.concatenate([high, high, low], axis=1)
    turns = np.concatenate([turn.real, turn.imag], axis=1).astype(np.float32)
    return fwd1, stack_k(fwd2), stack_k(inv2), inv1, turns


def dot(left, right, dims=None):
    if dims is None:
        return jnp.dot(left, right, preferred_element_type=F32)
    return lax.dot_general(left, right, dims, preferred_element_type=F32)


def split(value):
    high = value.astype(BF16)
    return high, (value - high.astype(F32)).astype(BF16)


def spectrum(columns, fwd1, fwd2, turn_r, turn_i):
    joined = jnp.concatenate(columns, axis=1)
    stage = dot(fwd1, jnp.concatenate([joined, joined], axis=0))
    rows = []
    for item in range(len(columns)):
        real = stage[:N1, N2 * item : N2 * (item + 1)]
        imag = stage[N1:, N2 * item : N2 * (item + 1)]
        turned = jnp.concatenate(
            [real * turn_r - imag * turn_i, real * turn_i + imag * turn_r], axis=1
        )
        high, low = split(turned)
        rows.append(jnp.concatenate([high, low, high], axis=1))
    done = dot(jnp.concatenate(rows, axis=0), fwd2)
    return [
        (done[N1 * i : N1 * (i + 1), :N2], done[N1 * i : N1 * (i + 1), N2:])
        for i in range(len(columns))
    ]


def positions(spectra, inv2, inv1, turn_r, turn_i):
    rows = []
    for real, imag in spectra:
        high, low = split(jnp.concatenate([real, imag], axis=1))
        rows.append(jnp.concatenate([high, low, high], axis=1))
    stage = dot(jnp.concatenate(rows, axis=0), inv2)
    columns = []
    for item in range(len(spectra)):
        real = stage[N1 * item : N1 * (item + 1), :N2]
        imag = stage[N1 * item : N1 * (item + 1), N2:]
        columns.append(
            jnp.concatenate(
                [real * turn_r + imag * turn_i, imag * turn_r - real * turn_i], axis=0
            )
        )
    high, low = split(jnp.concatenate(columns, axis=1))
    done = dot(inv1, jnp.concatenate([high, low, high], axis=0))
    return [done[:, N2 * i : N2 * (i + 1)] for i in range(len(spectra))]


def exchange_body(axis, size, count, *refs):
    sources, targets = refs[:count], refs[count : 2 * count]
    send_sem, recv_sem, own_sem = refs[2 * count :]
    me = lax.axis_index(axis)
    barrier = pltpu.get_barrier_semaphore()
    for step in range(1, size):
        pl.semaphore_signal(
            barrier,
            inc=1,
            device_id={axis: lax.rem(me + step, size)},
            device_id_type=pl.DeviceIdType.MESH,
        )
    own = [
        pltpu.make_async_copy(s.at[me], t.at[me], own_sem.at[i])
        for i, (s, t) in enumerate(zip(sources, targets))
    ]
    for copy in own:
        copy.start()
    pl.semaphore_wait(barrier, size - 1)
    copies = []
    for step in range(1, size):
        peer = lax.rem(me + step, size)
        for i, (s, t) in enumerate(zip(sources, targets)):
            copies.append(
                pltpu.make_async_remote_copy(
                    src_ref=s.at[peer],
                    dst_ref=t.at[me],
                    send_sem=send_sem.at[i, step],
                    recv_sem=recv_sem.at[i, step],
                    device_id={axis: peer},
                    device_id_type=pl.DeviceIdType.MESH,
                )
            )
            copies[-1].start()
    for copy in own:
        copy.wait()
    for copy in copies:
        copy.wait()


def exchange(arrays, axis, size, collective_id):
    count = len(arrays)
    return pl.pallas_call(
        functools.partial(exchange_body, axis, size, count),
        out_shape=[jax.ShapeDtypeStruct(a.shape, a.dtype) for a in arrays],
        in_specs=[VMEM] * count,
        out_specs=[VMEM] * count,
        scratch_shapes=[
            pltpu.SemaphoreType.DMA((count, size)),
            pltpu.SemaphoreType.DMA((count, size)),
            pltpu.SemaphoreType.DMA((count,)),
        ],
        compiler_params=pltpu.CompilerParams(
            collective_id=collective_id, has_side_effects=True, vmem_limit_bytes=LIMIT
        ),
        name=f"exchange_{collective_id}",
    )(*arrays)


def call(body, outs, scratch=(), specs=None, name=None):
    def run(*args):
        return pl.pallas_call(
            body,
            out_shape=[jax.ShapeDtypeStruct(s, d) for s, d in outs],
            in_specs=specs or [VMEM] * len(args),
            out_specs=[VMEM] * len(outs),
            scratch_shapes=list(scratch),
            compiler_params=pltpu.CompilerParams(vmem_limit_bytes=LIMIT),
            name=name,
        )(*args)

    return run


def to_rows(value, scratch):
    channels, length = value.shape
    units = length // 128
    for u in range(units):
        scratch[pl.ds(u, channels, stride=units), :] = value[:, 128 * u : 128 * (u + 1)]
    return scratch[...]


def prep_body(rows_ref, signal_ref, taps_ref, data_ref, ask_ref, place_ref, scratch):
    parts, kinds, own, units, width = data_ref.shape
    for kind, ref in enumerate((signal_ref, taps_ref)):
        flat = to_rows(ref[...].astype(F32), scratch).astype(BF16)
        data_ref[:, kind] = flat.reshape(parts, own, units, width)
    rows = rows_ref[...]
    groups = rows.shape[0]
    owner = rows >> 15
    high = ((rows >> 8) & 127).astype(F32)
    low = (rows & 255).astype(F32) + 1.0
    each = lax.broadcasted_iota(I32, (parts, 128), 0)
    onehots = [(owner[b : b + 1, :] == each).astype(F32) for b in range(groups)]
    stacked = jnp.concatenate(onehots, axis=0).astype(BF16)
    size = groups * parts
    above = lax.broadcasted_iota(I32, (128, 128), 0) < lax.broadcasted_iota(I32, (128, 128), 1)
    within = dot(stacked, above.astype(BF16))
    totals = dot(stacked, jnp.ones((128, 128), BF16))
    to, of = lax.broadcasted_iota(I32, (size, size), 0), lax.broadcasted_iota(I32, (size, size), 1)
    earlier = ((to - of) > 0) & (lax.rem(to + size - of, parts) == 0)
    rank = within + dot(earlier.astype(BF16), totals.astype(BF16))
    target = lax.broadcasted_iota(I32, (128, 128), 0).astype(F32)
    asked = jnp.zeros((2 * parts, 128), F32)
    for b in range(groups):
        mine = jnp.sum(onehots[b] * rank[parts * b : parts * (b + 1)], axis=0, keepdims=True)
        place_ref[b : b + 1, :] = owner[b : b + 1, :] * 128 + mine.astype(I32)
        ranks = (target == mine).astype(BF16)
        values = jnp.concatenate(
            [onehots[b] * high[b : b + 1, :], onehots[b] * low[b : b + 1, :]], axis=0
        )
        asked = asked + dot(values.astype(BF16), ranks, NT)
    asked = 256.0 * asked[:parts] + asked[parts:]
    for o in range(parts):
        ask_ref[o] = jnp.broadcast_to(asked[o : o + 1, :], (8, 128))


def lists(ask_ref):
    parts = ask_ref.shape[0]
    row = jnp.concatenate([ask_ref[s][0:1, :] for s in range(parts)], axis=1)
    row = row.astype(I32) - 1
    return row >> 8, row & 255


def forward_body(
    data_ref, ask_ref, table_ref, fwd1, fwd2, inv2, inv1, turns,
    conv_ref, found_ref, spec_ref, folded, picked,
):
    parts, kinds, own, units, width = data_ref.shape
    turn_r, turn_i = turns[:, :N2], turns[:, N2:]
    columns = [
        data_ref[:, kind, c].reshape(N1, N2) for kind in range(kinds) for c in range(own)
    ]
    spectra = spectrum(columns, fwd1[...], fwd2[...], turn_r, turn_i)
    for i, (real, imag) in enumerate(spectra):
        spec_ref[i, 0] = real
        spec_ref[i, 1] = imag
    products = []
    for c in range(own):
        (xr, xi), (hr, hi) = spectra[c], spectra[own + c]
        products.append((xr * hr - xi * hi, xr * hi + xi * hr))
    for c, value in enumerate(positions(products, inv2[...], inv1[...], turn_r, turn_i)):
        conv_ref[:, c] = value.astype(BF16).reshape(parts, units, width)

    channels = table_ref.shape[0]
    for h in range(128):
        folded[channels * h : channels * (h + 1), :] = table_ref[:, 256 * h : 256 * (h + 1)]
    high, low = lists(ask_ref)
    asked = high.shape[1]
    span, group = 256, 32
    for chunk in range(asked // span):
        cut = slice(span * chunk, span * (chunk + 1))
        onehot = lax.broadcasted_iota(I32, (256, span), 0) == low[:, cut]
        picked[...] = jnp.where(onehot, 1.0, 0.0).astype(BF16)
        row = jnp.broadcast_to(high[:, cut], (channels, span))

        def step(g, total):
            start = pl.multiple_of(g * group * channels, group * channels)
            all_high = dot(folded[pl.ds(start, group * channels), :], picked[...])
            for h in range(group):
                part = all_high[channels * h : channels * (h + 1)]
                total = total + jnp.where(row == g * group + h, part, 0.0)
            return total

        total = lax.fori_loop(0, 128 // group, step, jnp.zeros((channels, span), F32))
        for piece in range(span // 128):
            found_ref[chunk * (span // 128) + piece] = total[
                :, 128 * piece : 128 * (piece + 1)
            ].astype(BF16)


def onehot_places(place_ref, b, total):
    return jnp.where(
        lax.broadcasted_iota(I32, (total, 128), 0) == place_ref[b : b + 1, :], 1.0, 0.0
    ).astype(BF16)


def encode_body(
    scale, conv_ref, got_ref, place_ref, signal_ref, gate_ref, gain_ref, positive_ref,
    part_ref, pre_ref, enc_ref, embed_ref, scratch,
):
    channels, length = signal_ref.shape
    units = length // 128
    scratch[...] = conv_ref[...].reshape(channels * units, 128).astype(F32)
    parts = got_ref.shape[0]
    groups = place_ref.shape[0]
    rows = jnp.concatenate([got_ref[o] for o in range(parts)], axis=1)
    gain = gain_ref[...]
    for b in range(groups):
        embed = dot(rows, onehot_places(place_ref, b, parts * 128)).astype(BF16)
        embed_ref[:, 128 * b : 128 * (b + 1)] = embed
        tops = []
        for half in range(2):
            u = 2 * b + half
            cut = slice(128 * u, 128 * (u + 1))
            conv = scratch[pl.ds(u, channels, stride=units), :]
            pre = scale * conv + gain * signal_ref[:, cut].astype(F32)
            pre_ref[:, cut] = pre
            enc = (gate_ref[:, cut].astype(F32) * pre).astype(BF16)
            enc_ref[:, cut] = enc
            score = dot(embed, enc, TN)
            part_ref[b, 64 * half : 64 * (half + 1), :] = score[
                64 * half : 64 * (half + 1)
            ].astype(BF16)
            tops.append(
                jnp.sum(enc.astype(F32) * positive_ref[:, cut].astype(F32), axis=0, keepdims=True)
            )
        tops.append(jnp.zeros((14, 128), F32))
        part_ref[b, 128:, :] = jnp.concatenate(tops, axis=0).astype(BF16)


def weigh_body(scale, got_ref, out_ref):
    total = got_ref[0].astype(F32)
    for i in range(1, got_ref.shape[0]):
        total = total + got_ref[i].astype(F32)
    total = scale * total
    negative = total[:128]
    out_ref[:128, :] = (1.0 / (1.0 + jnp.exp(-negative))).astype(BF16)
    out_ref[128:, :] = (-1.0 / (1.0 + jnp.exp(total[128:]))).astype(BF16)


def back_body(
    scale, counts_ref, weight_ref, place_ref, embed_ref, enc_ref, pre_ref, gate_ref, positive_ref,
    send_ref, out_ref, grad_gate_ref, back_ref, scratch,
):
    channels, length = gate_ref.shape
    units = length // 128
    groups = place_ref.shape[0]
    parts = send_ref.shape[0]
    lane = lax.broadcasted_iota(I32, (channels, 128), 1)
    row = lax.broadcasted_iota(I32, (128, 128), 0)
    outgoing = jnp.zeros((channels, parts * 128), F32)
    for b in range(groups):
        limit = jnp.where(row < 64, counts_ref[2 * b], 64 + counts_ref[2 * b + 1])
        weight = jnp.where(row < limit, weight_ref[b, :128, :].astype(F32), 0.0).astype(BF16)
        top = weight_ref[b, 128:, :].astype(F32)
        embed = embed_ref[:, 128 * b : 128 * (b + 1)].astype(F32)
        slot = []
        for half in range(2):
            u = 2 * b + half
            cut = slice(128 * u, 128 * (u + 1))
            keep = (lane >= 64) if half else (lane < 64)
            masked = jnp.where(keep, embed, 0.0).astype(BF16)
            positive = positive_ref[:, cut].astype(F32)
            grad = scale * (top[half : half + 1, :] * positive + dot(masked, weight))
            grad_gate_ref[:, cut] = (grad * pre_ref[:, cut]).astype(BF16)
            back = grad * gate_ref[:, cut].astype(F32)
            back_ref[:, cut] = back
            scratch[pl.ds(u, channels, stride=units), :] = back
            slot.append(dot(enc_ref[:, cut], weight, NT))
        slot = (scale * jnp.where(lane < 64, slot[0], slot[1])).astype(BF16)
        outgoing = outgoing + dot(slot, onehot_places(place_ref, b, parts * 128), NT)
    for o in range(parts):
        out_ref[o] = outgoing[:, 128 * o : 128 * (o + 1)].astype(BF16)
    send_ref[...] = scratch[...].astype(BF16).reshape(send_ref.shape)


def lag_body(
    data_ref, spec_ref, fwd1, fwd2, inv2, inv1, turns, result_ref,
):
    parts, own, units, width = data_ref.shape
    turn_r, turn_i = turns[:, :N2], turns[:, N2:]
    columns = [data_ref[:, c].reshape(N1, N2) for c in range(own)]
    spectra = spectrum(columns, fwd1[...], fwd2[...], turn_r, turn_i)
    products = []
    for kind in (1, 0):
        for c in range(own):
            (br, bi), item = spectra[c], kind * own + c
            sr, si = spec_ref[item, 0], spec_ref[item, 1]
            products.append((sr * br + si * bi, sr * bi - si * br))
    for i, value in enumerate(positions(products, inv2[...], inv1[...], turn_r, turn_i)):
        result_ref[:, i // own, i % own] = value.astype(BF16).reshape(parts, units, width)


def table_body(in_ref, ask_ref, out_ref, columns):
    parts, channels, width = in_ref.shape
    high, low = lists(ask_ref)
    for s in range(parts):
        lows = jnp.broadcast_to(low[:, 128 * s : 128 * (s + 1)], (128, 128)).astype(F32).T
        lows = jnp.concatenate([lows, lows], axis=1)
        onehot = lows == lax.broadcasted_iota(I32, (128, 256), 1).astype(F32)
        columns[128 * s : 128 * (s + 1), :] = jnp.where(onehot, 1.0, 0.0).astype(BF16)
    values = jnp.concatenate([in_ref[s] for s in range(parts)], axis=1)
    row = jnp.broadcast_to(high.astype(F32).astype(BF16), values.shape)
    zero = jnp.zeros_like(values)
    group = 8

    @pl.loop(0, 128 // group)
    def _(g):
        base = (g * group).astype(F32)
        rows = [
            jnp.where(row == (base + h).astype(BF16), values, zero) for h in range(group)
        ]
        sums = dot(jnp.concatenate(rows, axis=0), columns[...])
        for h in range(group):
            start = pl.multiple_of((g * group + h) * 256, 256)
            out_ref[:, pl.ds(start, 256)] = sums[channels * h : channels * (h + 1)]


def last_body(scale, got_ref, back_ref, gain_ref, signal_ref, filter_ref, scratch):
    channels, length = back_ref.shape
    units = length // 128
    own = got_ref.shape[2]
    gain = gain_ref[...]
    for kind in range(2):
        scratch[kind] = got_ref[:, kind].reshape(channels * units, 128).astype(F32)
    for u in range(units):
        cut = slice(128 * u, 128 * (u + 1))
        rows = pl.ds(u, channels, stride=units)
        signal_ref[:, cut] = scale * scratch[0, rows, :] + gain * back_ref[:, cut]
        filter_ref[:, cut] = scale * scratch[1, rows, :]


def local(
    seq, chan, signal, gate_values, filter_taps, skip_gain, positive, item_table, item_row,
    negative_ids, block_counts,
):
    channels, length = signal.shape
    units, own = length // 128, channels // seq
    filter_scale, score_scale = (seq * length) ** -0.5, C**-0.5
    tables = [jnp.asarray(t) for t in transform_tables()]
    gain = jnp.broadcast_to(skip_gain[:, None], (channels, 128))
    rows = item_row[negative_ids].reshape(-1, 128)
    groups = rows.shape[0]
    flat = pltpu.VMEM((channels * units, 128), F32)

    data, ask, place = call(
        prep_body,
        [((seq, 2, own, units, 128), BF16), ((seq, 8, 128), F32), ((groups, 128), I32)],
        [flat],
        name="prep",
    )(rows, signal, filter_taps)
    data, ask = exchange([data, ask], "seq", seq, 1)
    conv, found, spec = call(
        forward_body,
        [
            ((seq, own, units, 128), BF16),
            ((seq, channels, 128), BF16),
            ((2 * own, 2, N1, N2), F32),
        ],
        [pltpu.VMEM((128 * channels, 256), BF16), pltpu.VMEM((256, 256), BF16)],
        name="forward",
    )(data, ask, item_table, *tables)
    conv, got = exchange([conv, found], "seq", seq, 2)
    part, pre, enc, embed = call(
        functools.partial(encode_body, filter_scale),
        [
            ((chan, 144, 128), BF16),
            ((channels, length), F32),
            ((channels, length), BF16),
            ((channels, groups * 128), BF16),
        ],
        [flat],
        name="encode",
    )(conv, got, place, signal, gate_values, gain, positive)
    (part,) = exchange([part], "chan", chan, 3)
    (weight,) = call(
        functools.partial(weigh_body, score_scale), [((144, 128), BF16)], name="weigh"
    )(part)
    (weight,) = exchange(
        [jnp.broadcast_to(weight[None], (chan, 144, 128))], "chan", chan, 4
    )
    send, out, grad_gate, back = call(
        functools.partial(back_body, score_scale),
        [
            ((seq, own, units, 128), BF16),
            ((seq, channels, 128), BF16),
            ((channels, length), BF16),
            ((channels, length), F32),
        ],
        [flat],
        specs=[SMEM] + [VMEM] * 7,
        name="back",
    )(block_counts, weight, place, embed, enc, pre, gate_values, positive)
    data, incoming = exchange([send, out], "seq", seq, 5)
    (result,) = call(lag_body, [((seq, 2, own, units, 128), BF16)], name="lag")(
        data, spec, *tables
    )
    (result,) = exchange([result], "seq", seq, 6)
    (grad_table,) = call(
        table_body,
        [((channels, item_table.shape[1]), F32)],
        [pltpu.VMEM((seq * 128, 256), BF16)],
        name="table",
    )(incoming, ask)
    grad_signal, grad_filter = call(
        functools.partial(last_body, filter_scale),
        [((channels, length), F32), ((channels, length), F32)],
        [pltpu.VMEM((2, channels * units, 128), F32)],
        name="last",
    )(result, back, gain)
    return grad_signal, grad_gate, grad_filter, grad_table


def solution(mesh):
    in_specs = (
        P("chan", "seq"),
        P("chan", "seq"),
        P("chan", "seq"),
        P("chan"),
        P("chan", "seq"),
        P("chan", "seq"),
        P(),
        P("seq", None),
        P("seq"),
    )
    out_specs = (P("chan", "seq"),) * 4
    body = functools.partial(local, mesh.shape["seq"], mesh.shape["chan"])
    return jax.shard_map(body, mesh=mesh, in_specs=in_specs, out_specs=out_specs, check_vma=False)
```

time: 673 us -> 129 us (0.19)
  the two profiles are of different devices: /device:TPU:96 before, /device:TPU:0 now
where the time goes in v1:
time: 129 us; the launch traced here: 128 us
  Pallas kernels  113 us (88%)
  local copies, waits for them, and re-layouts  13.5 us (10%)
    pallas_call x6, Pallas kernels, exchange(): pl.pallas_call(functools.partial(exchange_body, axis, size, count), out_s...  66.9 us
    pallas_call x8, Pallas kernels, run(): pl.pallas_call(body, out_shape=[jax.ShapeDtypeStruct(s, d) for s, d in ou...  46.5 us
    gather x1, local copies, waits for them, and re-layouts, local(): rows = item_row[negative_ids].reshape(-1, 128)  10.5 us

profile of v1, /device:TPU:0, one launch (start us, length us, event | category | flops | bytes accessed | tf_op | source)
XLA Modules:
  0.0 128.4 jit_solution(6360008429369829089)
XLA Ops:
  0.6 0.0 copy-start
  0.6 0.8 compare_select_fusion
  1.5 0.1 reshape.16
  1.6 0.7 copy-done
  2.2 0.0 copy-start.1
  2.2 10.5 %gather_fusion = s32[1024]{0:T(1024)} fusion(s32[524288]{0:T(1024)S(1)} %copy-done, s32[1024]{0:T(1024)S(1)} %broadcast_clamp_fusion), kind=kCustom, calls=%fused_computation | custom fusion | bytes 12288 | tf_op jit(solution)/shard_map/gather | solution.py:421
  12.8 0.0 copy-done.1
  12.8 0.7 broadcast_in_dim.7.gain_ref
  13.5 2.3 %prep.1 = (bf16[16,2,2,16,128]{4,3,2,1,0:T(8,128)(2,1)}, f32[16,8,128]{2,1,0:T(8,128)}, s32[8,128]{1,0:T(8,128)}) custom-call(s32[8,128]{1,0:T(8,128)} %bitcast.1, bf16[32,2048]{1,0:T(8,128)(2,1)} %signal_ref.3, f32[32,2048]{1,0:T(8,128)} %taps_ref.1), custom_call_target="tpu_custom_call" | custom-call | tf_op jit(solution)/shard_map/prep/pallas_call | solution.py:160
  15.8 13.3 %exchange_1.1 = (bf16[16,2,2,16,128]{4,3,2,1,0:T(8,128)(2,1)}, f32[16,8,128]{2,1,0:T(8,128)}) custom-call(bf16[16,2,2,16,128]{4,3,2,1,0:T(8,128)(2,1)} %get-tuple-element.26.refs_0_, f32[16,8,128]{2,1,0:T(8,128)} %get-tuple-element.27.refs_1_), custom_call_target="tpu_custom_call" | custom-call | tf_op jit(solution)/shard_map/exchange_1/pallas_call | solution.py:141
  29.0 16.3 %forward.1 = (bf16[16,2,16,128]{3,2,1,0:T(8,128)(2,1)}, bf16[16,32,128]{2,1,0:T(8,128)(2,1)}, f32[4,2,256,128]{3,2,1,0:T(8,128)}) custom-call(bf16[16,2,2,16,128]{4,3,2,1,0:T(8,128)(2,1)} %get-tuple-element.28.data_ref, f32[16,8,128]{2,1,0:T(8,128)} %get-tuple-element.29.ask_ref, bf16[32,32768]{1,0:T(8,128)(2,1)} %table_ref.1, ...), custom_call_target="tpu_custom_call" | custom-call | tf_op jit(solution)/shard_map/forward/pallas_call | solution.py:160
  45.3 11.1 %exchange_2.1 = (bf16[16,2,16,128]{3,2,1,0:T(8,128)(2,1)}, bf16[16,32,128]{2,1,0:T(8,128)(2,1)}) custom-call(bf16[16,2,16,128]{3,2,1,0:T(8,128)(2,1)} %get-tuple-element.30.refs_0_, bf16[16,32,128]{2,1,0:T(8,128)(2,1)} %get-tuple-element.31.refs_1_), custom_call_target="tpu_custom_call" | custom-call | tf_op jit(solution)/shard_map/exchange_2/pallas_call | solution.py:141
  56.4 4.3 %encode.1 = (bf16[8,144,128]{2,1,0:T(8,128)(2,1)}, f32[32,2048]{1,0:T(8,128)}, bf16[32,2048]{1,0:T(8,128)(2,1)}, bf16[32,1024]{1,0:T(8,128)(2,1)}) custom-call(bf16[16,2,16,128]{3,2,1,0:T(8,128)(2,1)} %get-tuple-element.32.conv_ref, bf16[16,32,128]{2,1,0:T(8,128)(2,1)} %get-tuple-element.33.got_ref, s32[8,128]{1,0:T(8,128)} %get-tuple-element.34.place_ref, ...), custom_call_target="tpu_custom_call" | custom-call | tf_op jit(solution)/shard_map/encode/pallas_call | solution.py:160
  60.7 11.1 %exchange_3.1.got_ref = bf16[8,144,128]{2,1,0:T(8,128)(2,1)} custom-call(bf16[8,144,128]{2,1,0:T(8,128)(2,1)} %get-tuple-element.35.refs_0_), custom_call_target="tpu_custom_call" | custom-call | tf_op jit(solution)/shard_map/exchange_3/pallas_call | solution.py:141
  71.8 1.6 %weigh.1 = bf16[144,128]{1,0:T(8,128)(2,1)} custom-call(bf16[8,144,128]{2,1,0:T(8,128)(2,1)} %exchange_3.1.got_ref), custom_call_target="tpu_custom_call" | custom-call | tf_op jit(solution)/shard_map/weigh/pallas_call | solution.py:160
  73.5 1.5 %broadcast_in_dim.8.refs_0_ = bf16[8,144,128]{2,1,0:T(8,128)(2,1)} broadcast(bf16[144,128]{1,0:T(8,128)(2,1)} %weigh.1), dimensions={1,2} | broadcast | bytes 331776 | tf_op jit(solution)/shard_map/broadcast_in_dim | solution.py:459
  75.0 9.1 %exchange_4.1.weight_ref = bf16[8,144,128]{2,1,0:T(8,128)(2,1)} custom-call(bf16[8,144,128]{2,1,0:T(8,128)(2,1)} %broadcast_in_dim.8.refs_0_), custom_call_target="tpu_custom_call" | custom-call | tf_op jit(solution)/shard_map/exchange_4/pallas_call | solution.py:141
  84.1 4.5 %back.1 = (bf16[16,2,16,128]{3,2,1,0:T(8,128)(2,1)}, bf16[16,32,128]{2,1,0:T(8,128)(2,1)}, bf16[32,2048]{1,0:T(8,128)(2,1)}, f32[32,2048]{1,0:T(8,128)}) custom-call(s32[16]{0:T(128)} %counts_ref.1, bf16[8,144,128]{2,1,0:T(8,128)(2,1)} %exchange_4.1.weight_ref, s32[8,128]{1,0:T(8,128)} %get-tuple-element.34.place_ref, ...), custom_call_target="tpu_custom_call" | custom-call | tf_op jit(solution)/shard_map/back/pallas_call | solution.py:160
  88.6 11.7 %exchange_5.1 = (bf16[16,2,16,128]{3,2,1,0:T(8,128)(2,1)}, bf16[16,32,128]{2,1,0:T(8,128)(2,1)}) custom-call(bf16[16,2,16,128]{3,2,1,0:T(8,128)(2,1)} %get-tuple-element.39.refs_0_, bf16[16,32,128]{2,1,0:T(8,128)(2,1)} %get-tuple-element.40.refs_1_), custom_call_target="tpu_custom_call" | custom-call | tf_op jit(solution)/shard_map/exchange_5/pallas_call | solution.py:141
  100.3 5.1 %lag.1.refs_0_ = bf16[16,2,2,16,128]{4,3,2,1,0:T(8,128)(2,1)} custom-call(bf16[16,2,16,128]{3,2,1,0:T(8,128)(2,1)} %get-tuple-element.41.data_ref, f32[4,2,256,128]{3,2,1,0:T(8,128)} %get-tuple-element.42.spec_ref, bf16[512,512]{1,0:T(8,128)(2,1)} %constant.14.clone.fwd1, bf16[768,256]{1,0:T(8,128)(2,1)} %constant.15.clone.fwd2, ...), custom_call_target="tpu_custom_call" | custom-call | tf_op jit(solution)/shard_map/lag/pallas_call | solution.py:160
  105.4 10.6 %exchange_6.1.got_ref = bf16[16,2,2,16,128]{4,3,2,1,0:T(8,128)(2,1)} custom-call(bf16[16,2,2,16,128]{4,3,2,1,0:T(8,128)(2,1)} %lag.1.refs_0_), custom_call_target="tpu_custom_call" | custom-call | tf_op jit(solution)/shard_map/exchange_6/pallas_call | solution.py:141
  116.0 2.0 %last.1 = (f32[32,2048]{1,0:T(8,128)}, f32[32,2048]{1,0:T(8,128)}) custom-call(bf16[16,2,2,16,128]{4,3,2,1,0:T(8,128)(2,1)} %exchange_6.1.got_ref, f32[32,2048]{1,0:T(8,128)} %get-tuple-element.43.back_ref, f32[32,128]{1,0:T(8,128)} %broadcast_in_dim.7.gain_ref), custom_call_target="tpu_custom_call" | custom-call | tf_op jit(solution)/shard_map/last/pallas_call | solution.py:160
  118.1 10.3 %table.1 = f32[32,32768]{1,0:T(8,128)} custom-call(bf16[16,32,128]{2,1,0:T(8,128)(2,1)} %get-tuple-element.47.in_ref, f32[16,8,128]{2,1,0:T(8,128)} %get-tuple-element.29.ask_ref), custom_call_target="tpu_custom_call" | custom-call | tf_op jit(solution)/shard_map/table/pallas_call | solution.py:160
  (1 shorter events, 0.0 us)
Async XLA Ops:
  0.6 1.6 %copy-start = (s32[524288]{0:T(1024)S(1)}, s32[524288]{0:T(1024)}, u32[]{:S(2)}) copy-start(s32[524288]{0:T(1024)} %param.20) | copy-start | bytes 6291460
  2.2 10.5 %copy-start.1 = (f32[32]{0:T(128)S(1)}, f32[32]{0:T(128)}, u32[]{:S(2)}) copy-start(f32[32]{0:T(128)} %param.17) | copy-start | bytes 388

commit v2 on v1

v2 whole, which is shorter than its diff:
```python
import functools

import jax
import jax.numpy as jnp
import ml_dtypes
import numpy as np
from jax import lax
from jax.experimental import pallas as pl
from jax.experimental.pallas import tpu as pltpu
from jax.sharding import PartitionSpec as P

C = 256
F32, BF16, I32 = jnp.float32, jnp.bfloat16, jnp.int32
VMEM = pl.BlockSpec(memory_space=pltpu.VMEM)
SMEM = pl.BlockSpec(memory_space=pltpu.SMEM)
N1, N2 = 256, 128
LIMIT = 56 * 1024 * 1024
NT = (((1,), (1,)), ((), ()))
TN = (((0,), (0,)), ((), ()))


def halves(matrix):
    high = matrix.astype(ml_dtypes.bfloat16)
    return high, (matrix - high.astype(np.float64)).astype(ml_dtypes.bfloat16)


def transform_tables():
    total = N1 * N2
    k1, n1 = np.arange(N1) + 0.25, np.arange(N1)
    n2 = np.arange(N2)
    first = np.exp(-2j * np.pi * np.outer(k1, n1) / N1)
    turn = np.exp(-2j * np.pi * np.outer(k1, n2) / total)
    last = np.exp(-2j * np.pi * np.outer(n2, n2) / N2)
    fwd1 = np.concatenate(halves(np.concatenate([first.real, first.imag])), axis=1)
    fwd2 = np.block([[last.real, last.imag], [-last.imag, last.real]])
    inv2 = np.block([[last.real, -last.imag], [last.imag, last.real]])
    inv1 = np.concatenate([first.real.T, first.imag.T], axis=1) / total

    def stack_k(matrix):
        high, low = halves(matrix)
        return np.concatenate([high, high, low])

    high, low = halves(inv1)
    inv1 = np.concatenate([high, high, low], axis=1)
    turns = np.concatenate([turn.real, turn.imag], axis=1).astype(np.float32)
    return fwd1, stack_k(fwd2), stack_k(inv2), inv1, turns


def dot(left, right, dims=None):
    if dims is None:
        return jnp.dot(left, right, preferred_element_type=F32)
    return lax.dot_general(left, right, dims, preferred_element_type=F32)


def split(value):
    high = value.astype(BF16)
    return high, (value - high.astype(F32)).astype(BF16)


def spectrum(columns, fwd1, fwd2, turn_r, turn_i):
    joined = jnp.concatenate(columns, axis=1)
    stage = dot(fwd1, jnp.concatenate([joined, joined], axis=0))
    rows = []
    for item in range(len(columns)):
        real = stage[:N1, N2 * item : N2 * (item + 1)]
        imag = stage[N1:, N2 * item : N2 * (item + 1)]
        turned = jnp.concatenate(
            [real * turn_r - imag * turn_i, real * turn_i + imag * turn_r], axis=1
        )
        high, low = split(turned)
        rows.append(jnp.concatenate([high, low, high], axis=1))
    done = dot(jnp.concatenate(rows, axis=0), fwd2)
    return [
        (done[N1 * i : N1 * (i + 1), :N2], done[N1 * i : N1 * (i + 1), N2:])
        for i in range(len(columns))
    ]


def positions(spectra, inv2, inv1, turn_r, turn_i):
    rows = []
    for real, imag in spectra:
        high, low = split(jnp.concatenate([real, imag], axis=1))
        rows.append(jnp.concatenate([high, low, high], axis=1))
    stage = dot(jnp.concatenate(rows, axis=0), inv2)
    columns = []
    for item in range(len(spectra)):
        real = stage[N1 * item : N1 * (item + 1), :N2]
        imag = stage[N1 * item : N1 * (item + 1), N2:]
        columns.append(
            jnp.concatenate(
                [real * turn_r + imag * turn_i, imag * turn_r - real * turn_i], axis=0
            )
        )
    high, low = split(jnp.concatenate(columns, axis=1))
    done = dot(inv1, jnp.concatenate([high, low, high], axis=0))
    return [done[:, N2 * i : N2 * (i + 1)] for i in range(len(spectra))]


class Exchange:
    def __init__(self, axis, size, source, target, sems, one_piece=False):
        self.axis, self.size, self.source, self.target = axis, size, source, target
        self.send_sem, self.recv_sem = sems
        self.one_piece = one_piece

    def copy(self, step):
        me = lax.axis_index(self.axis)
        peer = lax.rem(me + step, self.size)
        return pltpu.make_async_remote_copy(
            src_ref=self.source if self.one_piece else self.source.at[peer],
            dst_ref=self.target.at[me],
            send_sem=self.send_sem.at[step],
            recv_sem=self.recv_sem.at[step],
            device_id={self.axis: peer},
            device_id_type=pl.DeviceIdType.MESH,
        )

    def start(self):
        @pl.loop(1, self.size)
        def _(step):
            self.copy(step).start()

        me = lax.axis_index(self.axis)
        self.target[me] = self.source[...] if self.one_piece else self.source[me]

    def wait(self):
        @pl.loop(1, self.size)
        def _(step):
            self.copy(step).wait()


def to_rows(value, scratch):
    channels, length = value.shape
    units = length // 128
    for u in range(units):
        scratch[pl.ds(u, channels, stride=units), :] = value[:, 128 * u : 128 * (u + 1)]
    return scratch[...]


def requests(rows, ask_ref, place_ref):
    parts = ask_ref.shape[0]
    groups = rows.shape[0]
    owner = rows >> 15
    high = ((rows >> 8) & 127).astype(F32)
    low = (rows & 255).astype(F32) + 1.0
    each = lax.broadcasted_iota(I32, (parts, 128), 0)
    onehots = [(owner[b : b + 1, :] == each).astype(F32) for b in range(groups)]
    stacked = jnp.concatenate(onehots, axis=0).astype(BF16)
    size = groups * parts
    above = lax.broadcasted_iota(I32, (128, 128), 0) < lax.broadcasted_iota(I32, (128, 128), 1)
    within = dot(stacked, above.astype(BF16))
    totals = dot(stacked, jnp.ones((128, 128), BF16))
    to, of = lax.broadcasted_iota(I32, (size, size), 0), lax.broadcasted_iota(I32, (size, size), 1)
    earlier = ((to - of) > 0) & (lax.rem(to + size - of, parts) == 0)
    rank = within + dot(earlier.astype(BF16), totals.astype(BF16))
    target = lax.broadcasted_iota(I32, (128, 128), 0).astype(F32)
    asked = jnp.zeros((2 * parts, 128), F32)
    for b in range(groups):
        mine = jnp.sum(onehots[b] * rank[parts * b : parts * (b + 1)], axis=0, keepdims=True)
        place_ref[b : b + 1, :] = owner[b : b + 1, :] * 128 + mine.astype(I32)
        ranks = (target == mine).astype(BF16)
        values = jnp.concatenate(
            [onehots[b] * high[b : b + 1, :], onehots[b] * low[b : b + 1, :]], axis=0
        )
        asked = asked + dot(values.astype(BF16), ranks, NT)
    asked = 256.0 * asked[:parts] + asked[parts:]
    for o in range(parts):
        ask_ref[o] = jnp.broadcast_to(asked[o : o + 1, :], (8, 128))


def lists(ask_ref):
    parts = ask_ref.shape[0]
    row = jnp.concatenate([ask_ref[s][0:1, :] for s in range(parts)], axis=1)
    row = row.astype(I32) - 1
    return row >> 8, row & 255


def find_rows(ask_ref, table_ref, folded, picked, found_ref):
    channels = table_ref.shape[0]
    for h in range(128):
        folded[channels * h : channels * (h + 1), :] = table_ref[:, 256 * h : 256 * (h + 1)]
    high, low = lists(ask_ref)
    asked = high.shape[1]
    span, group = 256, 32
    for chunk in range(asked // span):
        cut = slice(span * chunk, span * (chunk + 1))
        onehot = lax.broadcasted_iota(I32, (256, span), 0) == low[:, cut]
        picked[...] = jnp.where(onehot, 1.0, 0.0).astype(BF16)
        row = jnp.broadcast_to(high[:, cut], (channels, span))

        def step(g, total):
            start = pl.multiple_of(g * group * channels, group * channels)
            all_high = dot(folded[pl.ds(start, group * channels), :], picked[...])
            for h in range(group):
                part = all_high[channels * h : channels * (h + 1)]
                total = total + jnp.where(row == g * group + h, part, 0.0)
            return total

        total = lax.fori_loop(0, 128 // group, step, jnp.zeros((channels, span), F32))
        for piece in range(span // 128):
            found_ref[chunk * (span // 128) + piece] = total[
                :, 128 * piece : 128 * (piece + 1)
            ].astype(BF16)


def onehot_places(place_ref, b, total):
    return jnp.where(
        lax.broadcasted_iota(I32, (total, 128), 0) == place_ref[b : b + 1, :], 1.0, 0.0
    ).astype(BF16)


def add_rows(in_ref, ask_ref, columns, sums_ref, out_ref, sems):
    parts, channels, width = in_ref.shape
    high, low = lists(ask_ref)
    for s in range(parts):
        lows = jnp.broadcast_to(low[:, 128 * s : 128 * (s + 1)], (128, 128)).astype(F32).T
        lows = jnp.concatenate([lows, lows], axis=1)
        onehot = lows == lax.broadcasted_iota(I32, (128, 256), 1).astype(F32)
        columns[128 * s : 128 * (s + 1), :] = jnp.where(onehot, 1.0, 0.0).astype(BF16)
    values = jnp.concatenate([in_ref[s] for s in range(parts)], axis=1)
    row = jnp.broadcast_to(high.astype(F32).astype(BF16), values.shape)
    zero = jnp.zeros_like(values)
    group = sums_ref.shape[2] // 256

    def copy(g):
        start = pl.multiple_of(g * group * 256, group * 256)
        return pltpu.make_async_copy(
            sums_ref.at[g], out_ref.at[:, pl.ds(start, group * 256)], sems.at[g]
        )

    @pl.loop(0, 128 // group)
    def _(g):
        base = (g * group).astype(F32)
        rows = [
            jnp.where(row == (base + h).astype(BF16), values, zero) for h in range(group)
        ]
        sums = dot(jnp.concatenate(rows, axis=0), columns[...])
        for h in range(group):
            sums_ref[g, :, 256 * h : 256 * (h + 1)] = sums[channels * h : channels * (h + 1)]
        copy(g).start()

    return copy


def step_body(
    seq, chan, filter_scale, score_scale,
    ids_ref, counts_ref, lanes_ref, signal_ref, gate_ref, taps_ref, gain_ref, positive_ref,
    fwd1, fwd2, inv2, inv1, turns, table_hbm, item_hbm,
    grad_signal_ref, grad_gate_ref, grad_filter_ref, grad_table_hbm,
    data_s, data_r, ask_s, ask_r, conv_s, conv_r, found_s, found_r, part_s, part_r, weight_s, weight_r,
    gback_s, gback_r, out_s, out_r, res_s, res_r,
    place, flat, pre, enc, embed, back, spec, picked_rows, item, table, folded, picked, columns, sums,
    send_sems, recv_sems, local_sems, out_sems,
):
    channels, length = signal_ref.shape
    units = length // 128
    own = channels // seq
    groups = place.shape[0]

    def sems(i):
        return send_sems.at[i], recv_sems.at[i]

    data_x = Exchange("seq", seq, data_s, data_r, sems(0))
    ask_x = Exchange("seq", seq, ask_s, ask_r, sems(1))
    conv_x = Exchange("seq", seq, conv_s, conv_r, sems(2))
    found_x = Exchange("seq", seq, found_s, found_r, sems(3))
    part_x = Exchange("chan", chan, part_s, part_r, sems(4))
    weight_x = Exchange("chan", chan, weight_s, weight_r, sems(5), one_piece=True)
    gback_x = Exchange("seq", seq, gback_s, gback_r, sems(6))
    out_x = Exchange("seq", seq, out_s, out_r, sems(7))
    res_x = Exchange("seq", seq, res_s, res_r, sems(8))

    barrier = pltpu.get_barrier_semaphore()
    for axis, size in (("seq", seq), ("chan", chan)):
        me = lax.axis_index(axis)
        for step in range(1, size):
            pl.semaphore_signal(
                barrier,
                inc=1,
                device_id={axis: lax.rem(me + step, size)},
                device_id_type=pl.DeviceIdType.MESH,
            )
    item_copy = pltpu.make_async_copy(item_hbm, item, local_sems.at[0])
    table_copy = pltpu.make_async_copy(table_hbm, table, local_sems.at[1])
    item_copy.start()
    table_copy.start()

    for kind, ref in enumerate((signal_ref, taps_ref)):
        value = to_rows(ref[...].astype(F32), flat).astype(BF16)
        data_s[:, kind] = value.reshape(seq, own, units, 128)
    pl.semaphore_wait(barrier, seq + chan - 2)
    data_x.start()

    item_copy.wait()
    per = ids_ref.shape[1]

    @pl.loop(0, ids_ref.shape[0])
    def _(u):
        for j in range(per):
            picked_rows[pl.ds(u * per + j, 1), :] = item[pl.ds(ids_ref[u, j] >> 7, 1), :]

    lane_at = lanes_ref[...] & 127
    rows = []
    for b in range(groups):
        block = picked_rows[128 * b : 128 * (b + 1), :].astype(F32).T
        here = lax.broadcasted_iota(I32, (128, 128), 0) == lane_at[b : b + 1, :]
        rows.append(jnp.sum(jnp.where(here, block, 0.0), axis=0, keepdims=True))
    requests(jnp.concatenate(rows, axis=0).astype(I32), ask_s, place)
    ask_x.start()

    turn_r, turn_i = turns[:, :N2], turns[:, N2:]
    data_x.wait()
    spectra = spectrum(
        [data_r[:, kind, c].reshape(N1, N2) for kind in range(2) for c in range(own)],
        fwd1[...], fwd2[...], turn_r, turn_i,
    )
    for i, (real, imag) in enumerate(spectra):
        spec[i, 0] = real
        spec[i, 1] = imag
    products = []
    for c in range(own):
        (xr, xi), (hr, hi) = spectra[c], spectra[own + c]
        products.append((xr * hr - xi * hi, xr * hi + xi * hr))
    for c, value in enumerate(positions(products, inv2[...], inv1[...], turn_r, turn_i)):
        conv_s[:, c] = value.astype(BF16).reshape(seq, units, 128)
    conv_x.start()

    ask_x.wait()
    table_copy.wait()
    find_rows(ask_r, table, folded, picked, found_s)
    found_x.start()

    conv_x.wait()
    flat[...] = conv_r[...].reshape(channels * units, 128).astype(F32)
    square = lax.broadcasted_iota(I32, (channels, channels), 0) == lax.broadcasted_iota(
        I32, (channels, channels), 1
    )
    gain = jnp.sum(jnp.where(square, gain_ref[...], 0.0), axis=1, keepdims=True)
    tops = []
    for u in range(units):
        cut = slice(128 * u, 128 * (u + 1))
        conv = flat[pl.ds(u, channels, stride=units), :]
        value = filter_scale * conv + gain * signal_ref[:, cut].astype(F32)
        pre[:, cut] = value
        coded = (gate_ref[:, cut].astype(F32) * value).astype(BF16)
        enc[:, cut] = coded
        tops.append(
            jnp.sum(coded.astype(F32) * positive_ref[:, cut].astype(F32), axis=0, keepdims=True)
        )
    for b in range(groups):
        top = jnp.concatenate(tops[2 * b : 2 * b + 2] + [jnp.zeros((14, 128), F32)], axis=0)
        part_s[b, 128:, :] = top.astype(BF16)

    found_x.wait()
    found = jnp.concatenate([found_r[o] for o in range(seq)], axis=1)
    for b in range(groups):
        got = dot(found, onehot_places(place, b, seq * 128)).astype(BF16)
        embed[:, 128 * b : 128 * (b + 1)] = got
        for half in range(2):
            u = 2 * b + half
            score = dot(got, enc[:, 128 * u : 128 * (u + 1)], TN)
            rows = slice(64 * half, 64 * (half + 1))
            part_s[b, rows, :] = score[rows].astype(BF16)
    part_x.start()

    part_x.wait()
    total = part_r[0].astype(F32)
    for i in range(1, chan):
        total = total + part_r[i].astype(F32)
    total = score_scale * total
    weight_s[:128, :] = (1.0 / (1.0 + jnp.exp(-total[:128]))).astype(BF16)
    weight_s[128:, :] = (-1.0 / (1.0 + jnp.exp(total[128:]))).astype(BF16)
    weight_x.start()

    weight_x.wait()
    lane = lax.broadcasted_iota(I32, (channels, 128), 1)
    line = lax.broadcasted_iota(I32, (128, 128), 0)
    weights = []
    for b in range(groups):
        limit = jnp.where(line < 64, counts_ref[2 * b], 64 + counts_ref[2 * b + 1])
        weight = jnp.where(line < limit, weight_r[b, :128, :].astype(F32), 0.0).astype(BF16)
        weights.append(weight)
        top = weight_r[b, 128:, :].astype(F32)
        wide = embed[:, 128 * b : 128 * (b + 1)].astype(F32)
        for half in range(2):
            u = 2 * b + half
            cut = slice(128 * u, 128 * (u + 1))
            masked = jnp.where((lane >= 64) if half else (lane < 64), wide, 0.0).astype(BF16)
            positive = positive_ref[:, cut].astype(F32)
            grad = score_scale * (top[half : half + 1, :] * positive + dot(masked, weight))
            grad_gate_ref[:, cut] = (grad * pre[:, cut]).astype(BF16)
            value = grad * gate_ref[:, cut].astype(F32)
            back[:, cut] = gain * value
            flat[pl.ds(u, channels, stride=units), :] = value
    gback_s[...] = flat[...].astype(BF16).reshape(gback_s.shape)
    gback_x.start()

    outgoing = jnp.zeros((channels, seq * 128), F32)
    for b in range(groups):
        slot = [
            dot(enc[:, 128 * u : 128 * (u + 1)], weights[b], NT) for u in (2 * b, 2 * b + 1)
        ]
        slot = (score_scale * jnp.where(lane < 64, slot[0], slot[1])).astype(BF16)
        outgoing = outgoing + dot(slot, onehot_places(place, b, seq * 128), NT)
    for o in range(seq):
        out_s[o] = outgoing[:, 128 * o : 128 * (o + 1)].astype(BF16)
    out_x.start()

    gback_x.wait()
    spectra = spectrum(
        [gback_r[:, c].reshape(N1, N2) for c in range(own)], fwd1[...], fwd2[...], turn_r, turn_i
    )
    products = []
    for kind in (1, 0):
        for c in range(own):
            (br, bi), at = spectra[c], kind * own + c
            sr, si = spec[at, 0], spec[at, 1]
            products.append((sr * br + si * bi, sr * bi - si * br))
    for i, value in enumerate(positions(products, inv2[...], inv1[...], turn_r, turn_i)):
        res_s[:, i // own, i % own] = value.astype(BF16).reshape(seq, units, 128)
    res_x.start()

    out_x.wait()
    copy = add_rows(out_r, ask_r, columns, sums, grad_table_hbm, out_sems)
    res_x.wait()
    for kind, ref in enumerate((grad_signal_ref, grad_filter_ref)):
        flat[...] = res_r[:, kind].reshape(channels * units, 128).astype(F32)
        for u in range(units):
            cut = slice(128 * u, 128 * (u + 1))
            value = filter_scale * flat[pl.ds(u, channels, stride=units), :]
            ref[:, cut] = value + back[:, cut] if kind == 0 else value

    @pl.loop(0, sums.shape[0])
    def _(g):
        copy(g).wait()


def local(
    seq, chan, signal, gate_values, filter_taps, skip_gain, positive, item_table, item_row,
    negative_ids, block_counts,
):
    channels, length = signal.shape
    units, own = length // 128, channels // seq
    rows_own = item_table.shape[1]
    slots = negative_ids.size
    groups = slots // 128
    table_groups = 4
    tables = [jnp.asarray(t) for t in transform_tables()]
    seq_pair = lambda *shape: [pltpu.VMEM((seq, *shape), BF16)] * 2
    scratch = [
        *seq_pair(2, own, units, 128),
        *[pltpu.VMEM((seq, 8, 128), F32)] * 2,
        *seq_pair(own, units, 128),
        *seq_pair(channels, 128),
        *[pltpu.VMEM((chan, 144, 128), BF16)] * 2,
        pltpu.VMEM((144, 128), BF16),
        pltpu.VMEM((chan, 144, 128), BF16),
        *seq_pair(own, units, 128),
        *seq_pair(channels, 128),
        *seq_pair(2, own, units, 128),
        pltpu.VMEM((groups, 128), I32),
        pltpu.VMEM((channels * units, 128), F32),
        pltpu.VMEM((channels, length), F32),
        pltpu.VMEM((channels, length), BF16),
        pltpu.VMEM((channels, slots), BF16),
        pltpu.VMEM((channels, length), F32),
        pltpu.VMEM((2 * own, 2, N1, N2), F32),
        pltpu.VMEM((slots, 128), I32),
        pltpu.VMEM((item_row.size // 128, 128), I32),
        pltpu.VMEM((channels, rows_own), BF16),
        pltpu.VMEM((channels * rows_own // 256, 256), BF16),
        pltpu.VMEM((256, 256), BF16),
        pltpu.VMEM((seq * 128, 256), BF16),
        pltpu.VMEM((table_groups, channels, rows_own // table_groups), F32),
        pltpu.SemaphoreType.DMA((9, seq)),
        pltpu.SemaphoreType.DMA((9, seq)),
        pltpu.SemaphoreType.DMA((2,)),
        pltpu.SemaphoreType.DMA((table_groups,)),
    ]
    any_space = pl.BlockSpec(memory_space=pl.ANY)
    return pl.pallas_call(
        functools.partial(step_body, seq, chan, (seq * length) ** -0.5, C**-0.5),
        out_shape=[
            jax.ShapeDtypeStruct((channels, length), F32),
            jax.ShapeDtypeStruct((channels, length), BF16),
            jax.ShapeDtypeStruct((channels, length), F32),
            jax.ShapeDtypeStruct((channels, rows_own), F32),
        ],
        in_specs=[SMEM] * 2 + [VMEM] * 11 + [any_space] * 2,
        out_specs=[VMEM] * 3 + [any_space],
        scratch_shapes=scratch,
        compiler_params=pltpu.CompilerParams(
            collective_id=1, has_side_effects=True, vmem_limit_bytes=LIMIT
        ),
        name="step",
    )(
        negative_ids, block_counts, negative_ids.reshape(groups, 128), signal, gate_values,
        filter_taps, skip_gain.reshape(1, channels), positive, *tables, item_table,
        item_row.reshape(-1, 128),
    )


def solution(mesh):
    in_specs = (
        P("chan", "seq"),
        P("chan", "seq"),
        P("chan", "seq"),
        P("chan"),
        P("chan", "seq"),
        P("chan", "seq"),
        P(),
        P("seq", None),
        P("seq"),
    )
    out_specs = (P("chan", "seq"),) * 4
    body = functools.partial(local, mesh.shape["seq"], mesh.shape["chan"])
    return jax.shard_map(body, mesh=mesh, in_specs=in_specs, out_specs=out_specs, check_vma=False)
```

time: 129 us -> 76 us (0.59)
  Pallas kernels: 113 us -> 64.2 us
  local copies, waits for them, and re-layouts: 13.5 us -> 10.7 us
    pallas_call x14 -> x1, Pallas kernels: 113 us -> 64.2 us  [local(): pl.pallas_call(functools.partial(step_body, seq, chan, (seq * length) **...]
    gather x1 -> x0, local copies, waits for them, and re-layouts: 10.5 us -> none  [local(): rows = item_row[negative_ids].reshape(-1, 128)]
    unnamed x4, local copies, waits for them, and re-layouts: 0.68 us -> 9.38 us
    broadcast_in_dim x3 -> x0, local copies, waits for them, and re-layouts: 2.26 us -> none  [the longest x1 1.52 us: local(): jnp.broadcast_to(weight[None], (chan, 144, 128))]
    reshape x0 -> x1, local copies, waits for them, and re-layouts: none -> 1.36 us  [local(): negative_ids.reshape(groups, 128)]
where the time goes in v2:
time: 76 us; the launch traced here: 75.6 us
  Pallas kernels  64.2 us (84%)
  local copies, waits for them, and re-layouts  10.7 us (14%)
    pallas_call x1, Pallas kernels, local(): pl.pallas_call(functools.partial(step_body, seq, chan, (seq * length) **...  64.2 us
    unnamed x4, local copies, waits for them, and re-layouts  9.38 us

profile of v2, /device:TPU:0, one launch (start us, length us, event | category | flops | bytes accessed | tf_op | source)
XLA Modules:
  0.0 75.6 jit_solution(6231320696217596043)
XLA Ops:
  0.6 1.4 %reshape.17.lanes_ref = s32[8,128]{1,0:T(8,128)} reshape(s32[16,64]{1,0:T(8,128)} %ids_ref.1) | data formatting | bytes 8192 | tf_op jit(solution)/shard_map/reshape | solution.py:496
  2.0 64.2 %step.1 = (f32[32,2048]{1,0:T(8,128)}, bf16[32,2048]{1,0:T(8,128)(2,1)}, f32[32,2048]{1,0:T(8,128)}, f32[32,32768]{1,0:T(8,128)}) custom-call(s32[16,64]{1,0:T(8,128)} %ids_ref.1, s32[16]{0:T(128)} %counts_ref.1, s32[8,128]{1,0:T(8,128)} %reshape.17.lanes_ref, bf16[32,2048]{1,0:T(8,128)(2,1)} %signal_ref.1, bf16[32,2048]{1,0:T(8,128)(2,1)} %gate_ref.1, ...), custom_call_target="tpu_custom_call" | custom-call | tf_op jit(solution)/shard_map/step/pallas_call | solution.py:480
  66.2 1.7 %copy.22 = f32[32,2048]{1,0:T(8,128)} copy(f32[32,2048]{1,0:T(8,128)} %get-tuple-element.8) | data formatting | bytes 524288
  67.8 1.6 %copy.23 = bf16[32,2048]{1,0:T(8,128)(2,1)} copy(bf16[32,2048]{1,0:T(8,128)(2,1)} %get-tuple-element.9) | data formatting | bytes 262144
  69.4 1.7 %copy.24 = f32[32,2048]{1,0:T(8,128)} copy(f32[32,2048]{1,0:T(8,128)} %get-tuple-element.10) | data formatting | bytes 524288
  71.1 4.5 %copy.25 = f32[32,32768]{1,0:T(8,128)} copy(f32[32,32768]{1,0:T(8,128)} %get-tuple-element.11) | data formatting | bytes 8388608

commit v3 on v2

--- a/solution.py
+++ b/solution.py
@@ -13,7 +13,10 @@
 F32, BF16, I32 = jnp.float32, jnp.bfloat16, jnp.int32
 VMEM = pl.BlockSpec(memory_space=pltpu.VMEM)
 SMEM = pl.BlockSpec(memory_space=pltpu.SMEM)
+ANY = pl.BlockSpec(memory_space=pl.ANY)
 N1, N2 = 256, 128
+LOW_BITS = 9
+LOW = 1 << LOW_BITS
 LIMIT = 56 * 1024 * 1024
 NT = (((1,), (1,)), ((), ()))
 TN = (((0,), (0,)), ((), ()))
@@ -136,7 +139,7 @@
     return scratch[...]
 
 
-def requests(rows, ask_ref, place_ref):
+def requests(rows, turned, ask_ref, place_ref):
     parts = ask_ref.shape[0]
     groups = rows.shape[0]
     owner = rows >> 15
@@ -156,8 +159,9 @@
     asked = jnp.zeros((2 * parts, 128), F32)
     for b in range(groups):
         mine = jnp.sum(onehots[b] * rank[parts * b : parts * (b + 1)], axis=0, keepdims=True)
-        place_ref[b : b + 1, :] = owner[b : b + 1, :] * 128 + mine.astype(I32)
-        ranks = (target == mine).astype(BF16)
+        at = (mine.astype(I32) + turned) & 127
+        place_ref[b : b + 1, :] = owner[b : b + 1, :] * 128 + at
+        ranks = (target == at.astype(F32)).astype(BF16)
         values = jnp.concatenate(
             [onehots[b] * high[b : b + 1, :], onehots[b] * low[b : b + 1, :]], axis=0
         )
@@ -167,23 +171,38 @@
         ask_ref[o] = jnp.broadcast_to(asked[o : o + 1, :], (8, 128))
 
 
+def packed(pieces):
+    lane = lax.broadcasted_iota(I32, pieces[0].shape, 1)
+    out = []
+    for first in range(0, len(pieces), 4):
+        p = pieces[first : first + 4]
+        out += [jnp.where(lane < cut, p[i], p[i + 1]) for i, cut in enumerate((96, 64, 32))]
+    return jnp.concatenate(out, axis=1)
+
+
+def unpacked(joined):
+    t = [joined[:, 128 * i : 128 * (i + 1)] for i in range(3)]
+    lane = lax.broadcasted_iota(I32, t[0].shape, 1)
+    return [t[0], jnp.where(lane < 96, t[1], t[0]), jnp.where(lane < 64, t[2], t[1]), t[2]]
+
+
 def lists(ask_ref):
-    parts = ask_ref.shape[0]
-    row = jnp.concatenate([ask_ref[s][0:1, :] for s in range(parts)], axis=1)
+    row = packed([ask_ref[s][0:1, :] for s in range(ask_ref.shape[0])])
     row = row.astype(I32) - 1
-    return row >> 8, row & 255
-
-
-def find_rows(ask_ref, table_ref, folded, picked, found_ref):
-    channels = table_ref.shape[0]
-    for h in range(128):
-        folded[channels * h : channels * (h + 1), :] = table_ref[:, 256 * h : 256 * (h + 1)]
+    return row >> LOW_BITS, row & (LOW - 1)
+
+
+def find_rows(ask_ref, table_ref, folded, picked, row_found, found_ref):
+    channels, rows_own = table_ref.shape
+    highs = rows_own // LOW
+    for h in range(highs):
+        folded[channels * h : channels * (h + 1), :] = table_ref[:, LOW * h : LOW * (h + 1)]
     high, low = lists(ask_ref)
     asked = high.shape[1]
-    span, group = 256, 32
+    span, group = 512, 32
     for chunk in range(asked // span):
         cut = slice(span * chunk, span * (chunk + 1))
-        onehot = lax.broadcasted_iota(I32, (256, span), 0) == low[:, cut]
+        onehot = lax.broadcasted_iota(I32, (LOW, span), 0) == low[:, cut]
         picked[...] = jnp.where(onehot, 1.0, 0.0).astype(BF16)
         row = jnp.broadcast_to(high[:, cut], (channels, span))
 
@@ -195,11 +214,13 @@
                 total = total + jnp.where(row == g * group + h, part, 0.0)
             return total
 
-        total = lax.fori_loop(0, 128 // group, step, jnp.zeros((channels, span), F32))
-        for piece in range(span // 128):
-            found_ref[chunk * (span // 128) + piece] = total[
-                :, 128 * piece : 128 * (piece + 1)
-            ].astype(BF16)
+        row_found[:, cut] = lax.fori_loop(
+            0, highs // group, step, jnp.zeros((channels, span), F32)
+        )
+    for first in range(0, found_ref.shape[0], 4):
+        pieces = unpacked(row_found[:, 96 * first : 96 * (first + 4)])
+        for i, piece in enumerate(pieces):
+            found_ref[first + i] = piece.astype(BF16)
 
 
 def onehot_places(place_ref, b, total):
@@ -211,23 +232,21 @@
 def add_rows(in_ref, ask_ref, columns, sums_ref, out_ref, sems):
     parts, channels, width = in_ref.shape
     high, low = lists(ask_ref)
-    for s in range(parts):
+    for s in range(low.shape[1] // 128):
         lows = jnp.broadcast_to(low[:, 128 * s : 128 * (s + 1)], (128, 128)).astype(F32).T
-        lows = jnp.concatenate([lows, lows], axis=1)
-        onehot = lows == lax.broadcasted_iota(I32, (128, 256), 1).astype(F32)
+        lows = jnp.concatenate([lows] * (LOW // 128), axis=1)
+        onehot = lows == lax.broadcasted_iota(I32, (128, LOW), 1).astype(F32)
         columns[128 * s : 128 * (s + 1), :] = jnp.where(onehot, 1.0, 0.0).astype(BF16)
-    values = jnp.concatenate([in_ref[s] for s in range(parts)], axis=1)
+    values = packed([in_ref[s].astype(F32) for s in range(parts)]).astype(BF16)
     row = jnp.broadcast_to(high.astype(F32).astype(BF16), values.shape)
     zero = jnp.zeros_like(values)
-    group = sums_ref.shape[2] // 256
+    groups = sums_ref.shape[0]
+    group = sums_ref.shape[2] // LOW
 
     def copy(g):
-        start = pl.multiple_of(g * group * 256, group * 256)
-        return pltpu.make_async_copy(
-            sums_ref.at[g], out_ref.at[:, pl.ds(start, group * 256)], sems.at[g]
-        )
-
-    @pl.loop(0, 128 // group)
+        return pltpu.make_async_copy(sums_ref.at[g], out_ref.at[g], sems.at[g])
+
+    @pl.loop(0, groups)
     def _(g):
         base = (g * group).astype(F32)
         rows = [
@@ -235,7 +254,7 @@
         ]
         sums = dot(jnp.concatenate(rows, axis=0), columns[...])
         for h in range(group):
-            sums_ref[g, :, 256 * h : 256 * (h + 1)] = sums[channels * h : channels * (h + 1)]
+            sums_ref[g, :, LOW * h : LOW * (h + 1)] = sums[channels * h : channels * (h + 1)]
         copy(g).start()
 
     return copy
@@ -243,14 +262,18 @@
 
 def step_body(
     seq, chan, filter_scale, score_scale,
-    ids_ref, counts_ref, lanes_ref, signal_ref, gate_ref, taps_ref, gain_ref, positive_ref,
-    fwd1, fwd2, inv2, inv1, turns, table_hbm, item_hbm,
-    grad_signal_ref, grad_gate_ref, grad_filter_ref, grad_table_hbm,
+    ids_ref, counts_ref, lanes_ref, signal_ref, taps_ref, gain_ref, *refs,
+):
+    later_hbm, refs = refs[:9], refs[9:]
+    lag_ref, back, grad_gate_ref, grad_table_hbm = refs[:4]
+    (
     data_s, data_r, ask_s, ask_r, conv_s, conv_r, found_s, found_r, part_s, part_r, weight_s, weight_r,
     gback_s, gback_r, out_s, out_r, res_s, res_r,
-    place, flat, pre, enc, embed, back, spec, picked_rows, item, table, folded, picked, columns, sums,
+    place, flat, pre, enc, embed, spec, picked_rows, folded, picked, row_found, columns, sums,
     send_sems, recv_sems, local_sems, out_sems,
-):
+    *later,
+    ) = refs[4:]
+    item, fwd1, fwd2, inv2, inv1, turns, gate_ref, positive_ref, table = later
     channels, length = signal_ref.shape
     units = length // 128
     own = channels // seq
@@ -279,10 +302,12 @@
                 device_id={axis: lax.rem(me + step, size)},
                 device_id_type=pl.DeviceIdType.MESH,
             )
-    item_copy = pltpu.make_async_copy(item_hbm, item, local_sems.at[0])
-    table_copy = pltpu.make_async_copy(table_hbm, table, local_sems.at[1])
-    item_copy.start()
-    table_copy.start()
+    loads = [
+        pltpu.make_async_copy(s, t, local_sems.at[i])
+        for i, (s, t) in enumerate(zip(later_hbm, later))
+    ]
+    for load in loads:
+        load.start()
 
     for kind, ref in enumerate((signal_ref, taps_ref)):
         value = to_rows(ref[...].astype(F32), flat).astype(BF16)
@@ -290,7 +315,7 @@
     pl.semaphore_wait(barrier, seq + chan - 2)
     data_x.start()
 
-    item_copy.wait()
+    loads[0].wait()
     per = ids_ref.shape[1]
 
     @pl.loop(0, ids_ref.shape[0])
@@ -298,15 +323,26 @@
         for j in range(per):
             picked_rows[pl.ds(u * per + j, 1), :] = item[pl.ds(ids_ref[u, j] >> 7, 1), :]
 
-    lane_at = lanes_ref[...] & 127
     rows = []
+    ids = lanes_ref[...].astype(F32)
+    lane_at = jnp.concatenate(
+        [
+            jnp.concatenate([ids[2 * b : 2 * b + 1], ids[2 * b + 1 : 2 * b + 2]], axis=1)
+            for b in range(groups)
+        ],
+        axis=0,
+    )
+    lane_at = lane_at.astype(I32) & 127
     for b in range(groups):
         block = picked_rows[128 * b : 128 * (b + 1), :].astype(F32).T
         here = lax.broadcasted_iota(I32, (128, 128), 0) == lane_at[b : b + 1, :]
         rows.append(jnp.sum(jnp.where(here, block, 0.0), axis=0, keepdims=True))
-    requests(jnp.concatenate(rows, axis=0).astype(I32), ask_s, place)
+    turned = (96 * lax.axis_index("seq")) & 127
+    requests(jnp.concatenate(rows, axis=0).astype(I32), turned, ask_s, place)
     ask_x.start()
 
+    for load in loads[1:6]:
+        load.wait()
     turn_r, turn_i = turns[:, :N2], turns[:, N2:]
     data_x.wait()
     spectra = spectrum(
@@ -325,8 +361,9 @@
     conv_x.start()
 
     ask_x.wait()
-    table_copy.wait()
-    find_rows(ask_r, table, folded, picked, found_s)
+    for load in loads[6:]:
+        load.wait()
+    find_rows(ask_r, table, folded, picked, row_found, found_s)
     found_x.start()
 
     conv_x.wait()
@@ -422,16 +459,48 @@
     out_x.wait()
     copy = add_rows(out_r, ask_r, columns, sums, grad_table_hbm, out_sems)
     res_x.wait()
-    for kind, ref in enumerate((grad_signal_ref, grad_filter_ref)):
-        flat[...] = res_r[:, kind].reshape(channels * units, 128).astype(F32)
-        for u in range(units):
-            cut = slice(128 * u, 128 * (u + 1))
-            value = filter_scale * flat[pl.ds(u, channels, stride=units), :]
-            ref[:, cut] = value + back[:, cut] if kind == 0 else value
+    lag_ref[...] = res_r[...]
 
     @pl.loop(0, sums.shape[0])
     def _(g):
         copy(g).wait()
+
+
+def last_body(
+    scale, lag_ref, back_ref, gate_ref, table_hbm,
+    grad_signal_ref, grad_gate_ref, grad_filter_ref, grad_table_hbm, flat, held, in_sems, out_sems,
+):
+    groups, _, width = table_hbm.shape
+    pieces, _, span = held.shape
+    loads, copies = [], []
+    for i in range(pieces):
+        g, start = divmod(span * i, width)
+        loads.append(
+            pltpu.make_async_copy(
+                table_hbm.at[g, :, start : start + span], held.at[i], in_sems.at[i]
+            )
+        )
+        copies.append(
+            pltpu.make_async_copy(
+                held.at[i], grad_table_hbm.at[:, span * i : span * (i + 1)], out_sems.at[i]
+            )
+        )
+    for load in loads:
+        load.start()
+    grad_gate_ref[...] = gate_ref[...]
+    channels, length = back_ref.shape
+    units = length // 128
+    for kind, ref in enumerate((grad_signal_ref, grad_filter_ref)):
+        flat[...] = lag_ref[:, kind].reshape(channels * units, 128).astype(F32)
+        for u in range(units):
+            cut = slice(128 * u, 128 * (u + 1))
+            value = scale * flat[pl.ds(u, channels, stride=units), :]
+            ref[:, cut] = value + back_ref[:, cut] if kind == 0 else value
+        for i in range(pieces // 2 * kind, pieces // 2 * (kind + 1)):
+            loads[i].wait()
+            copies[i].start()
+    for copy in copies:
+        copy.wait()
 
 
 def local(
@@ -443,8 +512,9 @@
     rows_own = item_table.shape[1]
     slots = negative_ids.size
     groups = slots // 128
-    table_groups = 4
+    table_groups = 2
     tables = [jnp.asarray(t) for t in transform_tables()]
+    later = [item_row.reshape(-1, 128), *tables, gate_values, positive, item_table]
     seq_pair = lambda *shape: [pltpu.VMEM((seq, *shape), BF16)] * 2
     scratch = [
         *seq_pair(2, own, units, 128),
@@ -462,41 +532,57 @@
         pltpu.VMEM((channels, length), F32),
         pltpu.VMEM((channels, length), BF16),
         pltpu.VMEM((channels, slots), BF16),
-        pltpu.VMEM((channels, length), F32),
         pltpu.VMEM((2 * own, 2, N1, N2), F32),
         pltpu.VMEM((slots, 128), I32),
-        pltpu.VMEM((item_row.size // 128, 128), I32),
-        pltpu.VMEM((channels, rows_own), BF16),
-        pltpu.VMEM((channels * rows_own // 256, 256), BF16),
-        pltpu.VMEM((256, 256), BF16),
-        pltpu.VMEM((seq * 128, 256), BF16),
+        pltpu.VMEM((channels * rows_own // LOW, LOW), BF16),
+        pltpu.VMEM((LOW, 512), BF16),
+        pltpu.VMEM((channels, seq * 96), F32),
+        pltpu.VMEM((seq * 96, LOW), BF16),
         pltpu.VMEM((table_groups, channels, rows_own // table_groups), F32),
         pltpu.SemaphoreType.DMA((9, seq)),
         pltpu.SemaphoreType.DMA((9, seq)),
-        pltpu.SemaphoreType.DMA((2,)),
+        pltpu.SemaphoreType.DMA((len(later),)),
         pltpu.SemaphoreType.DMA((table_groups,)),
+        *[pltpu.VMEM(a.shape, a.dtype) for a in later],
     ]
-    any_space = pl.BlockSpec(memory_space=pl.ANY)
+    lag, back, gate, table = pl.pallas_call(
+        functools.partial(step_body, seq, chan, (seq * length) ** -0.5, C**-0.5),
+        out_shape=[
+            jax.ShapeDtypeStruct((seq, 2, own, units, 128), BF16),
+            jax.ShapeDtypeStruct((channels, length), F32),
+            jax.ShapeDtypeStruct((channels, length), BF16),
+            jax.ShapeDtypeStruct((table_groups, channels, rows_own // table_groups), F32),
+        ],
+        in_specs=[SMEM] * 2 + [VMEM] * 4 + [ANY] * len(later),
+        out_specs=[VMEM] * 3 + [ANY],
+        scratch_shapes=scratch,
+        compiler_params=pltpu.CompilerParams(
+            collective_id=1, has_side_effects=True, vmem_limit_bytes=LIMIT
+        ),
+        name="step",
+    )(
+        negative_ids, block_counts, negative_ids, signal, filter_taps,
+        skip_gain.reshape(1, channels), *later,
+    )
     return pl.pallas_call(
-        functools.partial(step_body, seq, chan, (seq * length) ** -0.5, C**-0.5),
+        functools.partial(last_body, (seq * length) ** -0.5),
         out_shape=[
             jax.ShapeDtypeStruct((channels, length), F32),
             jax.ShapeDtypeStruct((channels, length), BF16),
             jax.ShapeDtypeStruct((channels, length), F32),
             jax.ShapeDtypeStruct((channels, rows_own), F32),
         ],
-        in_specs=[SMEM] * 2 + [VMEM] * 11 + [any_space] * 2,
-        out_specs=[VMEM] * 3 + [any_space],
-        scratch_shapes=scratch,
-        compiler_params=pltpu.CompilerParams(
-            collective_id=1, has_side_effects=True, vmem_limit_bytes=LIMIT
-        ),
-        name="step",
-    )(
-        negative_ids, block_counts, negative_ids.reshape(groups, 128), signal, gate_values,
-        filter_taps, skip_gain.reshape(1, channels), positive, *tables, item_table,
-        item_row.reshape(-1, 128),
-    )
+        in_specs=[VMEM] * 3 + [ANY],
+        out_specs=[VMEM] * 3 + [ANY],
+        scratch_shapes=[
+            pltpu.VMEM((channels * units, 128), F32),
+            pltpu.VMEM((8, channels, rows_own // 8), F32),
+            pltpu.SemaphoreType.DMA((8,)),
+            pltpu.SemaphoreType.DMA((8,)),
+        ],
+        compiler_params=pltpu.CompilerParams(vmem_limit_bytes=LIMIT),
+        name="last",
+    )(lag, back, gate, table)
 
 
 def solution(mesh):

time: 76 us -> 63.2 us (0.83)
  local copies, waits for them, and re-layouts: 10.7 us -> 0 us
  Pallas kernels: 64.2 us -> 62.4 us
    unnamed x4 -> x0, local copies, waits for them, and re-layouts: 9.38 us -> none
    pallas_call x1, Pallas kernels: 64.2 us -> 57 us  [local(): pl.pallas_call(functools.partial(step_body, seq, chan, (seq * length) **...]
    pallas_call x0 -> x1, Pallas kernels: none -> 5.47 us  [local(): pl.pallas_call(functools.partial(last_body, (seq * length) ** (-0.5)), ou...]
    reshape x1 -> x0, local copies, waits for them, and re-layouts: 1.36 us -> none  [local(): negative_ids.reshape(groups, 128)]
where the time goes in v3:
time: 63.2 us; the launch traced here: 63.1 us
  Pallas kernels  62.4 us (99%)
  between operations  0.64 us (1%)
    pallas_call x1, Pallas kernels, local(): pl.pallas_call(functools.partial(step_body, seq, chan, (seq * length) **...  57 us
    pallas_call x1, Pallas kernels, local(): pl.pallas_call(functools.partial(last_body, (seq * length) ** (-0.5)), ou...  5.47 us

profile of v3, /device:TPU:0, one launch (start us, length us, event | category | flops | bytes accessed | tf_op | source)
XLA Modules:
  0.0 63.1 jit_solution(8882349331342467657)
XLA Ops:
  0.6 57.0 %step.1 = (bf16[16,2,2,16,128]{4,3,2,1,0:T(8,128)(2,1)}, f32[32,2048]{1,0:T(8,128)}, bf16[32,2048]{1,0:T(8,128)(2,1)}, f32[2,32,16384]{2,1,0:T(8,128)}) custom-call(s32[16,64]{1,0:T(8,128)} %lanes_ref.1, s32[16]{0:T(128)} %counts_ref.1, s32[16,64]{1,0:T(8,128)} %lanes_ref.1, bf16[32,2048]{1,0:T(8,128)(2,1)} %signal_ref.1, f32[32,2048]{1,0:T(8,128)} %taps_ref.1, ...), custom_call_target="tpu_custom_call" | custom-call | tf_op jit(solution)/shard_map/step/pallas_call | solution.py:548
  57.6 5.5 %last.1 = (f32[32,2048]{1,0:T(8,128)}, bf16[32,2048]{1,0:T(8,128)(2,1)}, f32[32,2048]{1,0:T(8,128)}, f32[32,32768]{1,0:T(8,128)}) custom-call(bf16[16,2,2,16,128]{4,3,2,1,0:T(8,128)(2,1)} %get-tuple-element.8.lag_ref, f32[32,2048]{1,0:T(8,128)} %get-tuple-element.9.back_ref, bf16[32,2048]{1,0:T(8,128)(2,1)} %get-tuple-element.10.gate_ref, ...), custom_call_target="tpu_custom_call" | custom-call | tf_op jit(solution)/shard_map/last/pallas_call | solution.py:567

commit v4 on v3

--- a/solution.py
+++ b/solution.py
@@ -41,10 +41,10 @@
 
     def stack_k(matrix):
         high, low = halves(matrix)
-        return np.concatenate([high, high, low])
+        return np.concatenate([high, low])
 
     high, low = halves(inv1)
-    inv1 = np.concatenate([high, high, low], axis=1)
+    inv1 = np.concatenate([high, low], axis=1)
     turns = np.concatenate([turn.real, turn.imag], axis=1).astype(np.float32)
     return fwd1, stack_k(fwd2), stack_k(inv2), inv1, turns
 
@@ -55,14 +55,14 @@
     return lax.dot_general(left, right, dims, preferred_element_type=F32)
 
 
-def split(value):
-    high = value.astype(BF16)
-    return high, (value - high.astype(F32)).astype(BF16)
+def twice(value, axis):
+    value = value.astype(BF16)
+    return jnp.concatenate([value, value], axis=axis)
 
 
 def spectrum(columns, fwd1, fwd2, turn_r, turn_i):
     joined = jnp.concatenate(columns, axis=1)
-    stage = dot(fwd1, jnp.concatenate([joined, joined], axis=0))
+    stage = dot(fwd1, twice(joined, 0))
     rows = []
     for item in range(len(columns)):
         real = stage[:N1, N2 * item : N2 * (item + 1)]
@@ -70,8 +70,7 @@
         turned = jnp.concatenate(
             [real * turn_r - imag * turn_i, real * turn_i + imag * turn_r], axis=1
         )
-        high, low = split(turned)
-        rows.append(jnp.concatenate([high, low, high], axis=1))
+        rows.append(twice(turned, 1))
     done = dot(jnp.concatenate(rows, axis=0), fwd2)
     return [
         (done[N1 * i : N1 * (i + 1), :N2], done[N1 * i : N1 * (i + 1), N2:])
@@ -82,8 +81,7 @@
 def positions(spectra, inv2, inv1, turn_r, turn_i):
     rows = []
     for real, imag in spectra:
-        high, low = split(jnp.concatenate([real, imag], axis=1))
-        rows.append(jnp.concatenate([high, low, high], axis=1))
+        rows.append(twice(jnp.concatenate([real, imag], axis=1), 1))
     stage = dot(jnp.concatenate(rows, axis=0), inv2)
     columns = []
     for item in range(len(spectra)):
@@ -94,22 +92,20 @@
                 [real * turn_r + imag * turn_i, imag * turn_r - real * turn_i], axis=0
             )
         )
-    high, low = split(jnp.concatenate(columns, axis=1))
-    done = dot(inv1, jnp.concatenate([high, low, high], axis=0))
+    done = dot(inv1, twice(jnp.concatenate(columns, axis=1), 0))
     return [done[:, N2 * i : N2 * (i + 1)] for i in range(len(spectra))]
 
 
 class Exchange:
-    def __init__(self, axis, size, source, target, sems, one_piece=False):
+    def __init__(self, axis, size, source, target, sems):
         self.axis, self.size, self.source, self.target = axis, size, source, target
         self.send_sem, self.recv_sem = sems
-        self.one_piece = one_piece
 
     def copy(self, step):
         me = lax.axis_index(self.axis)
         peer = lax.rem(me + step, self.size)
         return pltpu.make_async_remote_copy(
-            src_ref=self.source if self.one_piece else self.source.at[peer],
+            src_ref=self.source.at[peer],
             dst_ref=self.target.at[me],
             send_sem=self.send_sem.at[step],
             recv_sem=self.recv_sem.at[step],
@@ -123,7 +119,7 @@
             self.copy(step).start()
 
         me = lax.axis_index(self.axis)
-        self.target[me] = self.source[...] if self.one_piece else self.source[me]
+        self.target[me] = self.source[me]
 
     def wait(self):
         @pl.loop(1, self.size)
@@ -186,21 +182,16 @@
     return [t[0], jnp.where(lane < 96, t[1], t[0]), jnp.where(lane < 64, t[2], t[1]), t[2]]
 
 
-def lists(ask_ref):
-    row = packed([ask_ref[s][0:1, :] for s in range(ask_ref.shape[0])])
-    row = row.astype(I32) - 1
-    return row >> LOW_BITS, row & (LOW - 1)
-
-
-def find_rows(ask_ref, table_ref, folded, picked, row_found, found_ref):
-    channels, rows_own = table_ref.shape
-    highs = rows_own // LOW
-    for h in range(highs):
-        folded[channels * h : channels * (h + 1), :] = table_ref[:, LOW * h : LOW * (h + 1)]
-    high, low = lists(ask_ref)
-    asked = high.shape[1]
+def lists(asked):
+    return asked >> LOW_BITS, asked & (LOW - 1)
+
+
+def find_rows(asked, folded, picked, row_found, found_ref):
+    channels = row_found.shape[0]
+    highs = folded.shape[0] // channels
+    high, low = lists(asked)
     span, group = 512, 32
-    for chunk in range(asked // span):
+    for chunk in range(high.shape[1] // span):
         cut = slice(span * chunk, span * (chunk + 1))
         onehot = lax.broadcasted_iota(I32, (LOW, span), 0) == low[:, cut]
         picked[...] = jnp.where(onehot, 1.0, 0.0).astype(BF16)
@@ -223,41 +214,24 @@
             found_ref[first + i] = piece.astype(BF16)
 
 
-def onehot_places(place_ref, b, total):
-    return jnp.where(
-        lax.broadcasted_iota(I32, (total, 128), 0) == place_ref[b : b + 1, :], 1.0, 0.0
-    ).astype(BF16)
-
-
-def add_rows(in_ref, ask_ref, columns, sums_ref, out_ref, sems):
-    parts, channels, width = in_ref.shape
-    high, low = lists(ask_ref)
+def low_columns(asked, columns):
+    high, low = lists(asked)
     for s in range(low.shape[1] // 128):
         lows = jnp.broadcast_to(low[:, 128 * s : 128 * (s + 1)], (128, 128)).astype(F32).T
         lows = jnp.concatenate([lows] * (LOW // 128), axis=1)
         onehot = lows == lax.broadcasted_iota(I32, (128, LOW), 1).astype(F32)
         columns[128 * s : 128 * (s + 1), :] = jnp.where(onehot, 1.0, 0.0).astype(BF16)
-    values = packed([in_ref[s].astype(F32) for s in range(parts)]).astype(BF16)
+
+
+def add_rows(asked, values, columns, first, group, sums_ref):
+    channels = values.shape[0]
+    high, _ = lists(asked)
     row = jnp.broadcast_to(high.astype(F32).astype(BF16), values.shape)
     zero = jnp.zeros_like(values)
-    groups = sums_ref.shape[0]
-    group = sums_ref.shape[2] // LOW
-
-    def copy(g):
-        return pltpu.make_async_copy(sums_ref.at[g], out_ref.at[g], sems.at[g])
-
-    @pl.loop(0, groups)
-    def _(g):
-        base = (g * group).astype(F32)
-        rows = [
-            jnp.where(row == (base + h).astype(BF16), values, zero) for h in range(group)
-        ]
-        sums = dot(jnp.concatenate(rows, axis=0), columns[...])
-        for h in range(group):
-            sums_ref[g, :, LOW * h : LOW * (h + 1)] = sums[channels * h : channels * (h + 1)]
-        copy(g).start()
-
-    return copy
+    rows = [jnp.where(row == jnp.asarray(first + h, BF16), values, zero) for h in range(group)]
+    sums = dot(jnp.concatenate(rows, axis=0), columns[...])
+    for h in range(group):
+        sums_ref[:, LOW * h : LOW * (h + 1)] = sums[channels * h : channels * (h + 1)]
 
 
 def step_body(
@@ -265,14 +239,14 @@
     ids_ref, counts_ref, lanes_ref, signal_ref, taps_ref, gain_ref, *refs,
 ):
     later_hbm, refs = refs[:9], refs[9:]
-    lag_ref, back, grad_gate_ref, grad_table_hbm = refs[:4]
+    lag_ref, back, grad_gate_ref, values_ref, asked_ref, half_hbm = refs[:6]
     (
-    data_s, data_r, ask_s, ask_r, conv_s, conv_r, found_s, found_r, part_s, part_r, weight_s, weight_r,
-    gback_s, gback_r, out_s, out_r, res_s, res_r,
-    place, flat, pre, enc, embed, spec, picked_rows, folded, picked, row_found, columns, sums,
-    send_sems, recv_sems, local_sems, out_sems,
+    data_s, data_r, ask_s, ask_r, conv_s, conv_r, found_s, found_r, enc_s, enc_r, embed_s, embed_r,
+    negs_s, negs_r, slot_s, slot_r, gback_s, gback_r, out_s, out_r, res_s, res_r,
+    place, flat, pre, spec, picked_rows, folded, picked, row_found, columns, sums, places,
+    send_sems, recv_sems, local_sems, out_sem,
     *later,
-    ) = refs[4:]
+    ) = refs[6:]
     item, fwd1, fwd2, inv2, inv1, turns, gate_ref, positive_ref, table = later
     channels, length = signal_ref.shape
     units = length // 128
@@ -286,11 +260,13 @@
     ask_x = Exchange("seq", seq, ask_s, ask_r, sems(1))
     conv_x = Exchange("seq", seq, conv_s, conv_r, sems(2))
     found_x = Exchange("seq", seq, found_s, found_r, sems(3))
-    part_x = Exchange("chan", chan, part_s, part_r, sems(4))
-    weight_x = Exchange("chan", chan, weight_s, weight_r, sems(5), one_piece=True)
-    gback_x = Exchange("seq", seq, gback_s, gback_r, sems(6))
-    out_x = Exchange("seq", seq, out_s, out_r, sems(7))
-    res_x = Exchange("seq", seq, res_s, res_r, sems(8))
+    enc_x = Exchange("chan", chan, enc_s, enc_r, sems(4))
+    embed_x = Exchange("chan", chan, embed_s, embed_r, sems(5))
+    negs_x = Exchange("chan", chan, negs_s, negs_r, sems(6))
+    slot_x = Exchange("chan", chan, slot_s, slot_r, sems(7))
+    gback_x = Exchange("seq", seq, gback_s, gback_r, sems(8))
+    out_x = Exchange("seq", seq, out_s, out_r, sems(9))
+    res_x = Exchange("seq", seq, res_s, res_r, sems(10))
 
     barrier = pltpu.get_barrier_semaphore()
     for axis, size in (("seq", seq), ("chan", chan)):
@@ -312,9 +288,6 @@
     for kind, ref in enumerate((signal_ref, taps_ref)):
         value = to_rows(ref[...].astype(F32), flat).astype(BF16)
         data_s[:, kind] = value.reshape(seq, own, units, 128)
-    pl.semaphore_wait(barrier, seq + chan - 2)
-    data_x.start()
-
     loads[0].wait()
     per = ids_ref.shape[1]
 
@@ -322,6 +295,9 @@
     def _(u):
         for j in range(per):
             picked_rows[pl.ds(u * per + j, 1), :] = item[pl.ds(ids_ref[u, j] >> 7, 1), :]
+
+    pl.semaphore_wait(barrier, seq + chan - 2)
+    data_x.start()
 
     rows = []
     ids = lanes_ref[...].astype(F32)
@@ -341,8 +317,10 @@
     requests(jnp.concatenate(rows, axis=0).astype(I32), turned, ask_s, place)
     ask_x.start()
 
-    for load in loads[1:6]:
+    for load in loads[1:]:
         load.wait()
+    for h in range(table.shape[1] // LOW):
+        folded[channels * h : channels * (h + 1), :] = table[:, LOW * h : LOW * (h + 1)]
     turn_r, turn_i = turns[:, :N2], turns[:, N2:]
     data_x.wait()
     spectra = spectrum(
@@ -361,9 +339,9 @@
     conv_x.start()
 
     ask_x.wait()
-    for load in loads[6:]:
-        load.wait()
-    find_rows(ask_r, table, folded, picked, row_found, found_s)
+    asked = packed([ask_r[s][0:1, :] for s in range(seq)]).astype(I32) - 1
+    asked_ref[...] = jnp.broadcast_to(asked, asked_ref.shape)
+    find_rows(asked, folded, picked, row_found, found_s)
     found_x.start()
 
     conv_x.wait()
@@ -379,65 +357,70 @@
         value = filter_scale * conv + gain * signal_ref[:, cut].astype(F32)
         pre[:, cut] = value
         coded = (gate_ref[:, cut].astype(F32) * value).astype(BF16)
-        enc[:, cut] = coded
+        enc_s[u // 2, :, 128 * (u % 2) : 128 * (u % 2 + 1)] = coded
         tops.append(
             jnp.sum(coded.astype(F32) * positive_ref[:, cut].astype(F32), axis=0, keepdims=True)
         )
+    enc_x.start()
     for b in range(groups):
         top = jnp.concatenate(tops[2 * b : 2 * b + 2] + [jnp.zeros((14, 128), F32)], axis=0)
-        part_s[b, 128:, :] = top.astype(BF16)
+        embed_s[b, channels:, :] = top.astype(BF16)
+        slot = lax.broadcasted_iota(I32, (seq * 128, 128), 0)
+        places[b] = jnp.where(slot == place[b : b + 1, :], 1.0, 0.0).astype(BF16)
 
     found_x.wait()
     found = jnp.concatenate([found_r[o] for o in range(seq)], axis=1)
     for b in range(groups):
-        got = dot(found, onehot_places(place, b, seq * 128)).astype(BF16)
-        embed[:, 128 * b : 128 * (b + 1)] = got
-        for half in range(2):
-            u = 2 * b + half
-            score = dot(got, enc[:, 128 * u : 128 * (u + 1)], TN)
-            rows = slice(64 * half, 64 * (half + 1))
-            part_s[b, rows, :] = score[rows].astype(BF16)
-    part_x.start()
-
-    part_x.wait()
-    total = part_r[0].astype(F32)
-    for i in range(1, chan):
-        total = total + part_r[i].astype(F32)
-    total = score_scale * total
-    weight_s[:128, :] = (1.0 / (1.0 + jnp.exp(-total[:128]))).astype(BF16)
-    weight_s[128:, :] = (-1.0 / (1.0 + jnp.exp(total[128:]))).astype(BF16)
-    weight_x.start()
-
-    weight_x.wait()
-    lane = lax.broadcasted_iota(I32, (channels, 128), 1)
+        embed_s[b, :channels, :] = dot(found, places[b]).astype(BF16)
+    embed_x.start()
+
+    low_columns(asked_ref[0:1, :], columns)
+    enc_x.wait()
+    coded = jnp.concatenate([enc_r[z] for z in range(chan)], axis=0)
     line = lax.broadcasted_iota(I32, (128, 128), 0)
-    weights = []
-    for b in range(groups):
-        limit = jnp.where(line < 64, counts_ref[2 * b], 64 + counts_ref[2 * b + 1])
-        weight = jnp.where(line < limit, weight_r[b, :128, :].astype(F32), 0.0).astype(BF16)
-        weights.append(weight)
-        top = weight_r[b, 128:, :].astype(F32)
-        wide = embed[:, 128 * b : 128 * (b + 1)].astype(F32)
-        for half in range(2):
-            u = 2 * b + half
-            cut = slice(128 * u, 128 * (u + 1))
-            masked = jnp.where((lane >= 64) if half else (lane < 64), wide, 0.0).astype(BF16)
-            positive = positive_ref[:, cut].astype(F32)
-            grad = score_scale * (top[half : half + 1, :] * positive + dot(masked, weight))
-            grad_gate_ref[:, cut] = (grad * pre[:, cut]).astype(BF16)
-            value = grad * gate_ref[:, cut].astype(F32)
-            back[:, cut] = gain * value
-            flat[pl.ds(u, channels, stride=units), :] = value
+    mine = 2 * lax.axis_index("chan")
+    limit = jnp.where(line < 64, counts_ref[mine], 64 + counts_ref[mine + 1])
+    embed_x.wait()
+    embed = jnp.concatenate([embed_r[z, :channels, :] for z in range(chan)], axis=0)
+    score = dot(embed, coded, TN)
+    score = score_scale * jnp.where(line < 64, score[:, :128], score[:, 128:])
+    weight = jnp.where(line < limit, 1.0 / (1.0 + jnp.exp(-score)), 0.0)
+    weight = jnp.concatenate(
+        [jnp.where(line < 64, weight, 0.0), jnp.where(line < 64, 0.0, weight)], axis=1
+    ).astype(BF16)
+    top = embed_r[0, channels:, :].astype(F32)
+    for z in range(1, chan):
+        top = top + embed_r[z, channels:, :].astype(F32)
+    top = -1.0 / (1.0 + jnp.exp(score_scale * top))
+    negs = dot(embed, weight).astype(BF16)
+    for z in range(chan):
+        negs_s[z, :channels, :] = negs[channels * z : channels * (z + 1)]
+        negs_s[z, channels:, :128] = top.astype(BF16)
+        negs_s[z, channels:, 128:] = top.astype(BF16)
+    negs_x.start()
+    slot = (score_scale * dot(coded, weight, NT)).astype(BF16)
+    for z in range(chan):
+        slot_s[z] = slot[channels * z : channels * (z + 1)]
+    slot_x.start()
+
+    negs_x.wait()
+    for u in range(units):
+        b, half = divmod(u, 2)
+        cut, side = slice(128 * u, 128 * (u + 1)), slice(128 * half, 128 * (half + 1))
+        top = negs_r[b, channels:, side].astype(F32)[half : half + 1, :]
+        positive = positive_ref[:, cut].astype(F32)
+        grad = score_scale * (top * positive + negs_r[b, :channels, side].astype(F32))
+        grad_gate_ref[:, cut] = (grad * pre[:, cut]).astype(BF16)
+        value = grad * gate_ref[:, cut].astype(F32)
+        back[:, cut] = gain * value
+        flat[pl.ds(u, channels, stride=units), :] = value
     gback_s[...] = flat[...].astype(BF16).reshape(gback_s.shape)
     gback_x.start()
 
+    slot_x.wait()
     outgoing = jnp.zeros((channels, seq * 128), F32)
     for b in range(groups):
-        slot = [
-            dot(enc[:, 128 * u : 128 * (u + 1)], weights[b], NT) for u in (2 * b, 2 * b + 1)
-        ]
-        slot = (score_scale * jnp.where(lane < 64, slot[0], slot[1])).astype(BF16)
-        outgoing = outgoing + dot(slot, onehot_places(place, b, seq * 128), NT)
+        outgoing = outgoing + dot(slot_r[b], places[b], NT)
     for o in range(seq):
         out_s[o] = outgoing[:, 128 * o : 128 * (o + 1)].astype(BF16)
     out_x.start()
@@ -457,37 +440,57 @@
     res_x.start()
 
     out_x.wait()
-    copy = add_rows(out_r, ask_r, columns, sums, grad_table_hbm, out_sems)
+    values_ref[...] = packed([out_r[s].astype(F32) for s in range(seq)]).astype(BF16)
+    half = sums.shape[1] // LOW
+    add_rows(asked_ref[0:1, :], values_ref[...], columns, 0, half, sums)
+    copy = pltpu.make_async_copy(sums, half_hbm, out_sem)
+    copy.start()
     res_x.wait()
     lag_ref[...] = res_r[...]
-
-    @pl.loop(0, sums.shape[0])
-    def _(g):
-        copy(g).wait()
+    copy.wait()
 
 
 def last_body(
-    scale, lag_ref, back_ref, gate_ref, table_hbm,
-    grad_signal_ref, grad_gate_ref, grad_filter_ref, grad_table_hbm, flat, held, in_sems, out_sems,
+    scale, lag_hbm, back_hbm, gate_hbm, values_ref, asked_ref, half_hbm,
+    grad_signal_ref, grad_gate_ref, grad_filter_ref, grad_table_hbm,
+    flat, columns, held, sums, lag_ref, back_ref, in_sems, out_sems,
 ):
-    groups, _, width = table_hbm.shape
     pieces, _, span = held.shape
     loads, copies = [], []
     for i in range(pieces):
-        g, start = divmod(span * i, width)
-        loads.append(
-            pltpu.make_async_copy(
-                table_hbm.at[g, :, start : start + span], held.at[i], in_sems.at[i]
-            )
-        )
+        cut = slice(span * i, span * (i + 1))
+        loads.append(pltpu.make_async_copy(half_hbm.at[:, cut], held.at[i], in_sems.at[i]))
+        copies.append(
+            pltpu.make_async_copy(held.at[i], grad_table_hbm.at[:, cut], out_sems.at[i])
+        )
+    for i in range(sums.shape[0]):
+        start = span * pieces + sums.shape[2] * i
         copies.append(
             pltpu.make_async_copy(
-                held.at[i], grad_table_hbm.at[:, span * i : span * (i + 1)], out_sems.at[i]
+                sums.at[i],
+                grad_table_hbm.at[:, start : start + sums.shape[2]],
+                out_sems.at[pieces + i],
             )
         )
-    for load in loads:
+    small = [
+        pltpu.make_async_copy(lag_hbm, lag_ref, in_sems.at[pieces]),
+        pltpu.make_async_copy(back_hbm, back_ref, in_sems.at[pieces + 1]),
+        pltpu.make_async_copy(gate_hbm, grad_gate_ref, in_sems.at[pieces + 2]),
+    ]
+    for load in loads + small:
         load.start()
-    grad_gate_ref[...] = gate_ref[...]
+    asked = asked_ref[0:1, :]
+    low_columns(asked, columns)
+    for i in range(pieces):
+        loads[i].wait()
+        copies[i].start()
+    group = sums.shape[2] // LOW
+    for i in range(sums.shape[0]):
+        first = span * pieces // LOW + group * i
+        add_rows(asked, values_ref[...], columns, first, group, sums.at[i])
+        copies[pieces + i].start()
+    for load in small:
+        load.wait()
     channels, length = back_ref.shape
     units = length // 128
     for kind, ref in enumerate((grad_signal_ref, grad_filter_ref)):
@@ -496,9 +499,6 @@
             cut = slice(128 * u, 128 * (u + 1))
             value = scale * flat[pl.ds(u, channels, stride=units), :]
             ref[:, cut] = value + back_ref[:, cut] if kind == 0 else value
-        for i in range(pieces // 2 * kind, pieces // 2 * (kind + 1)):
-            loads[i].wait()
-            copies[i].start()
     for copy in copies:
         copy.wait()
 
@@ -512,7 +512,9 @@
     rows_own = item_table.shape[1]
     slots = negative_ids.size
     groups = slots // 128
-    table_groups = 2
+    first_highs = 40
+    half = LOW * first_highs
+    rest = rows_own - half
     tables = [jnp.asarray(t) for t in transform_tables()]
     later = [item_row.reshape(-1, 128), *tables, gate_values, positive, item_table]
     seq_pair = lambda *shape: [pltpu.VMEM((seq, *shape), BF16)] * 2
@@ -521,40 +523,42 @@
         *[pltpu.VMEM((seq, 8, 128), F32)] * 2,
         *seq_pair(own, units, 128),
         *seq_pair(channels, 128),
-        *[pltpu.VMEM((chan, 144, 128), BF16)] * 2,
-        pltpu.VMEM((144, 128), BF16),
-        pltpu.VMEM((chan, 144, 128), BF16),
+        *[pltpu.VMEM((chan, channels, 256), BF16)] * 2,
+        *[pltpu.VMEM((chan, channels + 16, 128), BF16)] * 2,
+        *[pltpu.VMEM((chan, channels + 16, 256), BF16)] * 2,
+        *[pltpu.VMEM((chan, channels, 128), BF16)] * 2,
         *seq_pair(own, units, 128),
         *seq_pair(channels, 128),
         *seq_pair(2, own, units, 128),
         pltpu.VMEM((groups, 128), I32),
         pltpu.VMEM((channels * units, 128), F32),
         pltpu.VMEM((channels, length), F32),
-        pltpu.VMEM((channels, length), BF16),
-        pltpu.VMEM((channels, slots), BF16),
         pltpu.VMEM((2 * own, 2, N1, N2), F32),
         pltpu.VMEM((slots, 128), I32),
         pltpu.VMEM((channels * rows_own // LOW, LOW), BF16),
         pltpu.VMEM((LOW, 512), BF16),
         pltpu.VMEM((channels, seq * 96), F32),
         pltpu.VMEM((seq * 96, LOW), BF16),
-        pltpu.VMEM((table_groups, channels, rows_own // table_groups), F32),
-        pltpu.SemaphoreType.DMA((9, seq)),
-        pltpu.SemaphoreType.DMA((9, seq)),
+        pltpu.VMEM((channels, half), F32),
+        pltpu.VMEM((groups, seq * 128, 128), BF16),
+        pltpu.SemaphoreType.DMA((11, seq)),
+        pltpu.SemaphoreType.DMA((11, seq)),
         pltpu.SemaphoreType.DMA((len(later),)),
-        pltpu.SemaphoreType.DMA((table_groups,)),
+        pltpu.SemaphoreType.DMA,
         *[pltpu.VMEM(a.shape, a.dtype) for a in later],
     ]
-    lag, back, gate, table = pl.pallas_call(
+    moved = pl.pallas_call(
         functools.partial(step_body, seq, chan, (seq * length) ** -0.5, C**-0.5),
         out_shape=[
             jax.ShapeDtypeStruct((seq, 2, own, units, 128), BF16),
             jax.ShapeDtypeStruct((channels, length), F32),
             jax.ShapeDtypeStruct((channels, length), BF16),
-            jax.ShapeDtypeStruct((table_groups, channels, rows_own // table_groups), F32),
+            jax.ShapeDtypeStruct((channels, seq * 96), BF16),
+            jax.ShapeDtypeStruct((8, seq * 96), I32),
+            jax.ShapeDtypeStruct((channels, half), F32),
         ],
         in_specs=[SMEM] * 2 + [VMEM] * 4 + [ANY] * len(later),
-        out_specs=[VMEM] * 3 + [ANY],
+        out_specs=[VMEM] * 5 + [ANY],
         scratch_shapes=scratch,
         compiler_params=pltpu.CompilerParams(
             collective_id=1, has_side_effects=True, vmem_limit_bytes=LIMIT
@@ -572,17 +576,21 @@
             jax.ShapeDtypeStruct((channels, length), F32),
             jax.ShapeDtypeStruct((channels, rows_own), F32),
         ],
-        in_specs=[VMEM] * 3 + [ANY],
+        in_specs=[ANY] * 3 + [VMEM] * 2 + [ANY],
         out_specs=[VMEM] * 3 + [ANY],
         scratch_shapes=[
             pltpu.VMEM((channels * units, 128), F32),
-            pltpu.VMEM((8, channels, rows_own // 8), F32),
-            pltpu.SemaphoreType.DMA((8,)),
-            pltpu.SemaphoreType.DMA((8,)),
+            pltpu.VMEM((seq * 96, LOW), BF16),
+            pltpu.VMEM((4, channels, half // 4), F32),
+            pltpu.VMEM((2, channels, rest // 2), F32),
+            pltpu.VMEM((seq, 2, own, units, 128), BF16),
+            pltpu.VMEM((channels, length), F32),
+            pltpu.SemaphoreType.DMA((7,)),
+            pltpu.SemaphoreType.DMA((6,)),
         ],
         compiler_params=pltpu.CompilerParams(vmem_limit_bytes=LIMIT),
         name="last",
-    )(lag, back, gate, table)
+    )(*moved)
 
 
 def solution(mesh):

time: 63.2 us -> 59.8 us (0.946)
  Pallas kernels: 62.4 us -> 58.9 us
    pallas_call x1, Pallas kernels: 57 us -> 53.2 us  [local(): pl.pallas_call(functools.partial(step_body, seq, chan, (seq * length) **...]
where the time goes in v4:
time: 59.8 us; the launch traced here: 59.6 us
  Pallas kernels  58.9 us (98%)
  between operations  0.64 us (1%)
    pallas_call x1, Pallas kernels, local(): pl.pallas_call(functools.partial(step_body, seq, chan, (seq * length) **...  53.2 us
    pallas_call x1, Pallas kernels, local(): pl.pallas_call(functools.partial(last_body, (seq * length) ** (-0.5)), ou...  5.77 us

profile of v4, /device:TPU:0, one launch (start us, length us, event | category | flops | bytes accessed | tf_op | source)
XLA Modules:
  0.0 59.6 jit_solution(2372043034677413385)
XLA Ops:
  0.6 53.2 %step.1 = (bf16[16,2,2,16,128]{4,3,2,1,0:T(8,128)(2,1)}, f32[32,2048]{1,0:T(8,128)}, bf16[32,2048]{1,0:T(8,128)(2,1)}, bf16[32,1536]{1,0:T(8,128)(2,1)}, s32[8,1536]{1,0:T(8,128)}, /*index=5*/f32[32,20480]{1,0:T(8,128)}) custom-call(s32[16,64]{1,0:T(8,128)} %lanes_ref.1, s32[16]{0:T(128)} %counts_ref.1, s32[16,64]{1,0:T(8,128)} %lanes_ref.1, ...), custom_call_target="tpu_custom_call" | custom-call | tf_op jit(solution)/shard_map/step/pallas_call | solution.py:550
  53.8 5.8 %last.1 = (f32[32,2048]{1,0:T(8,128)}, bf16[32,2048]{1,0:T(8,128)(2,1)}, f32[32,2048]{1,0:T(8,128)}, f32[32,32768]{1,0:T(8,128)}) custom-call(bf16[16,2,2,16,128]{4,3,2,1,0:T(8,128)(2,1)} %get-tuple-element.10.lag_hbm, f32[32,2048]{1,0:T(8,128)} %get-tuple-element.11.back_hbm, bf16[32,2048]{1,0:T(8,128)(2,1)} %get-tuple-element.12.gate_hbm, ...), custom_call_target="tpu_custom_call" | custom-call | tf_op jit(solution)/shard_map/last/pallas_call | solution.py:571

commit v5 on v4

--- a/solution.py
+++ b/solution.py
@@ -236,18 +236,21 @@
 
 def step_body(
     seq, chan, filter_scale, score_scale,
-    ids_ref, counts_ref, lanes_ref, signal_ref, taps_ref, gain_ref, *refs,
+    ids_ref, counts_ref, *refs,
 ):
-    later_hbm, refs = refs[:9], refs[9:]
-    lag_ref, back, grad_gate_ref, values_ref, asked_ref, half_hbm = refs[:6]
+    later_hbm, refs = refs[:13], refs[13:]
+    *moved_hbm, half_hbm = refs[:6]
     (
     data_s, data_r, ask_s, ask_r, conv_s, conv_r, found_s, found_r, enc_s, enc_r, embed_s, embed_r,
     negs_s, negs_r, slot_s, slot_r, gback_s, gback_r, out_s, out_r, res_s, res_r,
     place, flat, pre, spec, picked_rows, folded, picked, row_found, columns, sums, places,
-    send_sems, recv_sems, local_sems, out_sem,
+    send_sems, recv_sems, local_sems, out_sems, back, gate_grad, values_ref, asked_ref,
     *later,
     ) = refs[6:]
-    item, fwd1, fwd2, inv2, inv1, turns, gate_ref, positive_ref, table = later
+    (
+        signal_ref, taps_ref, item, lanes_ref, gain_ref, fwd1, fwd2, inv2, inv1, turns,
+        gate_ref, positive_ref, table,
+    ) = later
     channels, length = signal_ref.shape
     units = length // 128
     own = channels // seq
@@ -285,10 +288,15 @@
     for load in loads:
         load.start()
 
+    outs = [
+        pltpu.make_async_copy(s, t, out_sems.at[i])
+        for i, (s, t) in enumerate(zip((res_r, back, gate_grad, values_ref, asked_ref), moved_hbm))
+    ]
     for kind, ref in enumerate((signal_ref, taps_ref)):
+        loads[kind].wait()
         value = to_rows(ref[...].astype(F32), flat).astype(BF16)
         data_s[:, kind] = value.reshape(seq, own, units, 128)
-    loads[0].wait()
+    loads[2].wait()
     per = ids_ref.shape[1]
 
     @pl.loop(0, ids_ref.shape[0])
@@ -300,6 +308,7 @@
     data_x.start()
 
     rows = []
+    loads[3].wait()
     ids = lanes_ref[...].astype(F32)
     lane_at = jnp.concatenate(
         [
@@ -317,7 +326,7 @@
     requests(jnp.concatenate(rows, axis=0).astype(I32), turned, ask_s, place)
     ask_x.start()
 
-    for load in loads[1:]:
+    for load in loads[4:]:
         load.wait()
     for h in range(table.shape[1] // LOW):
         folded[channels * h : channels * (h + 1), :] = table[:, LOW * h : LOW * (h + 1)]
@@ -341,6 +350,7 @@
     ask_x.wait()
     asked = packed([ask_r[s][0:1, :] for s in range(seq)]).astype(I32) - 1
     asked_ref[...] = jnp.broadcast_to(asked, asked_ref.shape)
+    outs[4].start()
     find_rows(asked, folded, picked, row_found, found_s)
     found_x.start()
 
@@ -410,12 +420,14 @@
         top = negs_r[b, channels:, side].astype(F32)[half : half + 1, :]
         positive = positive_ref[:, cut].astype(F32)
         grad = score_scale * (top * positive + negs_r[b, :channels, side].astype(F32))
-        grad_gate_ref[:, cut] = (grad * pre[:, cut]).astype(BF16)
+        gate_grad[:, cut] = (grad * pre[:, cut]).astype(BF16)
         value = grad * gate_ref[:, cut].astype(F32)
         back[:, cut] = gain * value
         flat[pl.ds(u, channels, stride=units), :] = value
     gback_s[...] = flat[...].astype(BF16).reshape(gback_s.shape)
     gback_x.start()
+    outs[1].start()
+    outs[2].start()
 
     slot_x.wait()
     outgoing = jnp.zeros((channels, seq * 128), F32)
@@ -441,19 +453,29 @@
 
     out_x.wait()
     values_ref[...] = packed([out_r[s].astype(F32) for s in range(seq)]).astype(BF16)
-    half = sums.shape[1] // LOW
-    add_rows(asked_ref[0:1, :], values_ref[...], columns, 0, half, sums)
-    copy = pltpu.make_async_copy(sums, half_hbm, out_sem)
-    copy.start()
+    outs[3].start()
+    groups, _, span = sums.shape
+    halves = [
+        pltpu.make_async_copy(
+            sums.at[g], half_hbm.at[:, span * g : span * (g + 1)], out_sems.at[len(outs) + g]
+        )
+        for g in range(groups)
+    ]
+    group = span // LOW
+    for g in range(groups):
+        add_rows(asked_ref[0:1, :], values_ref[...], columns, group * g, group, sums.at[g])
+        halves[g].start()
     res_x.wait()
-    lag_ref[...] = res_r[...]
-    copy.wait()
+    outs[0].start()
+    for copy in outs + halves:
+        copy.wait()
 
 
 def last_body(
-    scale, lag_hbm, back_hbm, gate_hbm, values_ref, asked_ref, half_hbm,
-    grad_signal_ref, grad_gate_ref, grad_filter_ref, grad_table_hbm,
-    flat, columns, held, sums, lag_ref, back_ref, in_sems, out_sems,
+    scale, lag_hbm, back_hbm, gate_hbm, values_hbm, asked_hbm, half_hbm,
+    grad_signal_hbm, grad_gate_hbm, grad_filter_hbm, grad_table_hbm,
+    flat, columns, held, sums, lag_ref, back_ref, gate_ref, values_ref, asked_ref, results,
+    in_sems, out_sems,
 ):
     pieces, _, span = held.shape
     loads, copies = [], []
@@ -473,33 +495,54 @@
             )
         )
     small = [
-        pltpu.make_async_copy(lag_hbm, lag_ref, in_sems.at[pieces]),
-        pltpu.make_async_copy(back_hbm, back_ref, in_sems.at[pieces + 1]),
-        pltpu.make_async_copy(gate_hbm, grad_gate_ref, in_sems.at[pieces + 2]),
-    ]
-    for load in loads + small:
+        pltpu.make_async_copy(source, target, in_sems.at[pieces + i])
+        for i, (source, target) in enumerate(
+            (
+                (asked_hbm, asked_ref),
+                (values_hbm, values_ref),
+                (gate_hbm, gate_ref),
+                (lag_hbm, lag_ref),
+                (back_hbm, back_ref),
+            )
+        )
+    ]
+    for load in small[:2] + loads + small[2:]:
         load.start()
+    ends = [
+        pltpu.make_async_copy(source, target, out_sems.at[len(copies) + i])
+        for i, (source, target) in enumerate(
+            (
+                (results.at[0], grad_signal_hbm),
+                (results.at[1], grad_filter_hbm),
+                (gate_ref, grad_gate_hbm),
+            )
+        )
+    ]
+    small[0].wait()
     asked = asked_ref[0:1, :]
     low_columns(asked, columns)
     for i in range(pieces):
         loads[i].wait()
         copies[i].start()
+    small[1].wait()
     group = sums.shape[2] // LOW
     for i in range(sums.shape[0]):
         first = span * pieces // LOW + group * i
         add_rows(asked, values_ref[...], columns, first, group, sums.at[i])
         copies[pieces + i].start()
-    for load in small:
+    for load in small[2:]:
         load.wait()
+    ends[2].start()
     channels, length = back_ref.shape
     units = length // 128
-    for kind, ref in enumerate((grad_signal_ref, grad_filter_ref)):
+    for kind in range(2):
         flat[...] = lag_ref[:, kind].reshape(channels * units, 128).astype(F32)
         for u in range(units):
             cut = slice(128 * u, 128 * (u + 1))
             value = scale * flat[pl.ds(u, channels, stride=units), :]
-            ref[:, cut] = value + back_ref[:, cut] if kind == 0 else value
-    for copy in copies:
+            results[kind, :, cut] = value + back_ref[:, cut] if kind == 0 else value
+        ends[kind].start()
+    for copy in copies + ends:
         copy.wait()
 
 
@@ -512,11 +555,14 @@
     rows_own = item_table.shape[1]
     slots = negative_ids.size
     groups = slots // 128
-    first_highs = 40
+    first_highs = 48
     half = LOW * first_highs
     rest = rows_own - half
     tables = [jnp.asarray(t) for t in transform_tables()]
-    later = [item_row.reshape(-1, 128), *tables, gate_values, positive, item_table]
+    later = [
+        signal, filter_taps, item_row.reshape(-1, 128), negative_ids, skip_gain.reshape(1, channels),
+        *tables, gate_values, positive, item_table,
+    ]
     seq_pair = lambda *shape: [pltpu.VMEM((seq, *shape), BF16)] * 2
     scratch = [
         *seq_pair(2, own, units, 128),
@@ -539,12 +585,16 @@
         pltpu.VMEM((LOW, 512), BF16),
         pltpu.VMEM((channels, seq * 96), F32),
         pltpu.VMEM((seq * 96, LOW), BF16),
-        pltpu.VMEM((channels, half), F32),
+        pltpu.VMEM((3, channels, half // 3), F32),
         pltpu.VMEM((groups, seq * 128, 128), BF16),
         pltpu.SemaphoreType.DMA((11, seq)),
         pltpu.SemaphoreType.DMA((11, seq)),
         pltpu.SemaphoreType.DMA((len(later),)),
-        pltpu.SemaphoreType.DMA,
+        pltpu.SemaphoreType.DMA((8,)),
+        pltpu.VMEM((channels, length), F32),
+        pltpu.VMEM((channels, length), BF16),
+        pltpu.VMEM((channels, seq * 96), BF16),
+        pltpu.VMEM((8, seq * 96), I32),
         *[pltpu.VMEM(a.shape, a.dtype) for a in later],
     ]
     moved = pl.pallas_call(
@@ -557,17 +607,14 @@
             jax.ShapeDtypeStruct((8, seq * 96), I32),
             jax.ShapeDtypeStruct((channels, half), F32),
         ],
-        in_specs=[SMEM] * 2 + [VMEM] * 4 + [ANY] * len(later),
-        out_specs=[VMEM] * 5 + [ANY],
+        in_specs=[SMEM] * 2 + [ANY] * len(later),
+        out_specs=[ANY] * 6,
         scratch_shapes=scratch,
         compiler_params=pltpu.CompilerParams(
             collective_id=1, has_side_effects=True, vmem_limit_bytes=LIMIT
         ),
         name="step",
-    )(
-        negative_ids, block_counts, negative_ids, signal, filter_taps,
-        skip_gain.reshape(1, channels), *later,
-    )
+    )(negative_ids, block_counts, *later)
     return pl.pallas_call(
         functools.partial(last_body, (seq * length) ** -0.5),
         out_shape=[
@@ -576,8 +623,8 @@
             jax.ShapeDtypeStruct((channels, length), F32),
             jax.ShapeDtypeStruct((channels, rows_own), F32),
         ],
-        in_specs=[ANY] * 3 + [VMEM] * 2 + [ANY],
-        out_specs=[VMEM] * 3 + [ANY],
+        in_specs=[ANY] * 6,
+        out_specs=[ANY] * 4,
         scratch_shapes=[
             pltpu.VMEM((channels * units, 128), F32),
             pltpu.VMEM((seq * 96, LOW), BF16),
@@ -585,8 +632,12 @@
             pltpu.VMEM((2, channels, rest // 2), F32),
             pltpu.VMEM((seq, 2, own, units, 128), BF16),
             pltpu.VMEM((channels, length), F32),
-            pltpu.SemaphoreType.DMA((7,)),
-            pltpu.SemaphoreType.DMA((6,)),
+            pltpu.VMEM((channels, length), BF16),
+            pltpu.VMEM((channels, seq * 96), BF16),
+            pltpu.VMEM((8, seq * 96), I32),
+            pltpu.VMEM((2, channels, length), F32),
+            pltpu.SemaphoreType.DMA((9,)),
+            pltpu.SemaphoreType.DMA((9,)),
         ],
         compiler_params=pltpu.CompilerParams(vmem_limit_bytes=LIMIT),
         name="last",

time: 59.8 us -> 57.8 us (0.967)
  Pallas kernels: 58.9 us -> 57 us
    pallas_call x1, Pallas kernels: 5.77 us -> 4.08 us  [local(): pl.pallas_call(functools.partial(last_body, (seq * length) ** (-0.5)), ou...]
where the time goes in v5:
time: 57.8 us; the launch traced here: 57.6 us
  Pallas kernels  57 us (99%)
  between operations  0.64 us (1%)
    pallas_call x1, Pallas kernels, local(): pl.pallas_call(functools.partial(step_body, seq, chan, (seq * length) **...  52.9 us
    pallas_call x1, Pallas kernels, local(): pl.pallas_call(functools.partial(last_body, (seq * length) ** (-0.5)), ou...  4.08 us

profile of v5, /device:TPU:0, one launch (start us, length us, event | category | flops | bytes accessed | tf_op | source)
XLA Modules:
  0.0 57.6 jit_solution(6388105114182244204)
XLA Ops:
  0.6 52.9 %step.1 = (bf16[16,2,2,16,128]{4,3,2,1,0:T(8,128)(2,1)}, f32[32,2048]{1,0:T(8,128)}, bf16[32,2048]{1,0:T(8,128)(2,1)}, bf16[32,1536]{1,0:T(8,128)(2,1)}, s32[8,1536]{1,0:T(8,128)}, /*index=5*/f32[32,24576]{1,0:T(8,128)}) custom-call(s32[16,64]{1,0:T(8,128)} %refs_3_.1, s32[16]{0:T(128)} %counts_ref.1, bf16[32,2048]{1,0:T(8,128)(2,1)} %refs_0_.1, ...), custom_call_target="tpu_custom_call" | custom-call | tf_op jit(solution)/shard_map/step/pallas_call | solution.py:600
  53.6 4.1 %last.1 = (f32[32,2048]{1,0:T(8,128)}, bf16[32,2048]{1,0:T(8,128)(2,1)}, f32[32,2048]{1,0:T(8,128)}, f32[32,32768]{1,0:T(8,128)}) custom-call(bf16[16,2,2,16,128]{4,3,2,1,0:T(8,128)(2,1)} %get-tuple-element.10.lag_hbm, f32[32,2048]{1,0:T(8,128)} %get-tuple-element.11.back_hbm, bf16[32,2048]{1,0:T(8,128)(2,1)} %get-tuple-element.12.gate_hbm, ...), custom_call_target="tpu_custom_call" | custom-call | tf_op jit(solution)/shard_map/last/pallas_call | solution.py:618

commit v6 on v5

--- a/solution.py
+++ b/solution.py
@@ -107,8 +107,8 @@
         return pltpu.make_async_remote_copy(
             src_ref=self.source.at[peer],
             dst_ref=self.target.at[me],
-            send_sem=self.send_sem.at[step],
-            recv_sem=self.recv_sem.at[step],
+            send_sem=self.send_sem,
+            recv_sem=self.recv_sem,
             device_id={self.axis: peer},
             device_id_type=pl.DeviceIdType.MESH,
         )
@@ -122,9 +122,15 @@
         self.target[me] = self.source[me]
 
     def wait(self):
-        @pl.loop(1, self.size)
-        def _(step):
-            self.copy(step).wait()
+        me = lax.axis_index(self.axis)
+        pltpu.make_async_remote_copy(
+            src_ref=self.source.at[pl.ds(0, self.size - 1)],
+            dst_ref=self.target.at[pl.ds(0, self.size - 1)],
+            send_sem=self.send_sem,
+            recv_sem=self.recv_sem,
+            device_id={self.axis: lax.rem(me + 1, self.size)},
+            device_id_type=pl.DeviceIdType.MESH,
+        ).wait()
 
 
 def to_rows(value, scratch):
@@ -587,8 +593,8 @@
         pltpu.VMEM((seq * 96, LOW), BF16),
         pltpu.VMEM((3, channels, half // 3), F32),
         pltpu.VMEM((groups, seq * 128, 128), BF16),
-        pltpu.SemaphoreType.DMA((11, seq)),
-        pltpu.SemaphoreType.DMA((11, seq)),
+        pltpu.SemaphoreType.DMA((11,)),
+        pltpu.SemaphoreType.DMA((11,)),
         pltpu.SemaphoreType.DMA((len(later),)),
         pltpu.SemaphoreType.DMA((8,)),
         pltpu.VMEM((channels, length), F32),

time: 57.8 us -> 54.6 us (0.945)
  Pallas kernels: 57 us -> 53.8 us
    pallas_call x1, Pallas kernels: 52.9 us -> 49.7 us  [local(): pl.pallas_call(functools.partial(step_body, seq, chan, (seq * length) **...]
where the time goes in v6:
time: 54.6 us; the launch traced here: 54.5 us
  Pallas kernels  53.8 us (99%)
  between operations  0.64 us (1%)
    pallas_call x1, Pallas kernels, local(): pl.pallas_call(functools.partial(step_body, seq, chan, (seq * length) **...  49.7 us
    pallas_call x1, Pallas kernels, local(): pl.pallas_call(functools.partial(last_body, (seq * length) ** (-0.5)), ou...  4.09 us

profile of v6, /device:TPU:0, one launch (start us, length us, event | category | flops | bytes accessed | tf_op | source)
XLA Modules:
  0.0 54.5 jit_solution(8179119498870615238)
XLA Ops:
  0.6 49.7 %step.1 = (bf16[16,2,2,16,128]{4,3,2,1,0:T(8,128)(2,1)}, f32[32,2048]{1,0:T(8,128)}, bf16[32,2048]{1,0:T(8,128)(2,1)}, bf16[32,1536]{1,0:T(8,128)(2,1)}, s32[8,1536]{1,0:T(8,128)}, /*index=5*/f32[32,24576]{1,0:T(8,128)}) custom-call(s32[16,64]{1,0:T(8,128)} %refs_3_.1, s32[16]{0:T(128)} %counts_ref.1, bf16[32,2048]{1,0:T(8,128)(2,1)} %refs_0_.1, ...), custom_call_target="tpu_custom_call" | custom-call | tf_op jit(solution)/shard_map/step/pallas_call | solution.py:606
  50.4 4.1 %last.1 = (f32[32,2048]{1,0:T(8,128)}, bf16[32,2048]{1,0:T(8,128)(2,1)}, f32[32,2048]{1,0:T(8,128)}, f32[32,32768]{1,0:T(8,128)}) custom-call(bf16[16,2,2,16,128]{4,3,2,1,0:T(8,128)(2,1)} %get-tuple-element.10.lag_hbm, f32[32,2048]{1,0:T(8,128)} %get-tuple-element.11.back_hbm, bf16[32,2048]{1,0:T(8,128)(2,1)} %get-tuple-element.12.gate_hbm, ...), custom_call_target="tpu_custom_call" | custom-call | tf_op jit(solution)/shard_map/last/pallas_call | solution.py:624
